TPU v7x, 128 devices: a whole 4x4x4 slice. The times are simulated.
128 devices in a mesh: rollout: 4 (over y_lo, core), row: 8 (over x, y_hi), col: 4 (over z).
Axes of the slice: x: 4, y: 4 (y_hi: 2, y_lo: 2; y = y_hi * 2 + y_lo), z: 4, core: 2. Of those that a mesh axis runs over, the one named last changes fastest.
Arguments:
- queries: bfloat16 [16384, 4096], P(('rollout', 'row', 'col')), may hold values from -16 to 16
- keys: bfloat16 [16384, 512], P(('rollout', 'row', 'col')), may hold values from -16 to 16
- values: bfloat16 [16384, 512], P(('rollout', 'row', 'col')), may hold values from -6 to 6
- out_grad: bfloat16 [16384, 4096], P(('rollout', 'row', 'col')), may hold values from -12 to 12
- hidden_in: bfloat16 [16384, 8192], P(('rollout', 'col'), 'row'), may hold values from -1.5 to 1.5
- q_weight: bfloat16 [4096, 8192], P('col', 'row'), may hold values from -0.09375 to 0.09375
- lengths: int32 [4, 32], P('rollout'), may hold values from 1 to 256, 4096 in all within a row
- kv_order: int32 [4], replicated, may hold values from 0 to 3, each once
Outputs:
- key_grad: float32 [16384, 512], P(('rollout', 'row', 'col'))
- value_grad: float32 [16384, 512], P(('rollout', 'row', 'col'))
- input_grad: bfloat16 [16384, 8192], P(('rollout', 'col'), 'row')
- weight_grad: float32 [4096, 8192], P(('rollout', 'col'), 'row')
Inputs may be any that keep to these rules, and one draw needn't show every extreme that they name: `lengths`: each row lists, for 16 packed rollouts in order, a prompt length and then a response length; a row sums to 4096 and its largest entry is exactly 256. `kv_order`: A permutation of the 4 key-value heads.
All inputs are finite; a program needn't handle non-finite values.
Results may differ from a plain program's by a relative error of at most 0.0057.
Values may be sent and summed in bfloat16 or wider, within the bound.
No kernel may reach another device: no remote copies, remote signals or barrier semaphores. Data moves between devices by JAX's collectives and lax.ppermute only.
A program may use at most 192 MiB of HBM per device.

v0:
```python
import math

import jax
import jax.numpy as jnp
from jax import lax
from jax.sharding import PartitionSpec as P

HQ = 32
KV = 4
HD = 128
ROLLS = 16


def token_parts(lengths_row, length_total):
    bounds = jnp.cumsum(lengths_row)
    position = jnp.arange(length_total, dtype=jnp.int32)
    return jnp.sum((position[:, None] >= bounds[None, :]).astype(jnp.int32), axis=1)


def attend_head(query_all, key_all, value_all, grad_all, document, row_block, reach):
    length_total = query_all.shape[0]
    scale_factor = 1.0 / math.sqrt(query_all.shape[1])
    position = jnp.arange(length_total, dtype=jnp.int32)
    grad_key = jnp.zeros(key_all.shape, jnp.float32)
    grad_value = jnp.zeros(value_all.shape, jnp.float32)
    query_pieces = []
    for row_begin in range(0, length_total, row_block):
        row_end = row_begin + row_block
        key_first = max(0, row_begin - reach)
        query_rows = query_all[row_begin:row_end]
        grad_rows = grad_all[row_begin:row_end]
        key_rows = key_all[key_first:row_end]
        value_rows = value_all[key_first:row_end]
        allowed = (position[None, key_first:row_end] <= position[row_begin:row_end, None]) & (
            document[None, key_first:row_end] == document[row_begin:row_end, None]
        )
        raw_scores = (
            jnp.einsum("qd,kd->qk", query_rows, key_rows, preferred_element_type=jnp.float32)
            * scale_factor
        )
        raw_scores = jnp.where(allowed, raw_scores, -jnp.inf)
        row_top = jnp.max(raw_scores, axis=1, keepdims=True)
        exp_scores = jnp.exp(raw_scores - row_top)
        attention = exp_scores / jnp.sum(exp_scores, axis=1, keepdims=True)
        attention_half = attention.astype(jnp.bfloat16)
        grad_value = grad_value.at[key_first:row_end].add(
            jnp.einsum("qk,qd->kd", attention_half, grad_rows, preferred_element_type=jnp.float32)
        )
        grad_attention = jnp.einsum(
            "qd,kd->qk", grad_rows, value_rows, preferred_element_type=jnp.float32
        )
        row_delta = jnp.sum(attention * grad_attention, axis=1, keepdims=True)
        grad_scores = (attention * (grad_attention - row_delta) * scale_factor).astype(jnp.bfloat16)
        query_pieces.append(
            jnp.dot(grad_scores, key_rows, preferred_element_type=jnp.float32).astype(jnp.bfloat16)
        )
        grad_key = grad_key.at[key_first:row_end].add(
            jnp.einsum("qk,qd->kd", grad_scores, query_rows, preferred_element_type=jnp.float32)
        )
    return (jnp.concatenate(query_pieces, axis=0), grad_key, grad_value)


def body(queries, keys, values, out_grad, hidden_in, q_weight, lengths, kv_order):
    group_size = lax.axis_size(("row", "col"))
    rows_count = lax.axis_size("row")
    columns_count = lax.axis_size("col")
    token_dev = queries.shape[0]
    length_total = token_dev * group_size
    heads_dev = HQ // group_size
    sources_each = HQ // KV // heads_dev
    reach = 2 * (length_total // ROLLS)
    head_query, head_grad = (
        lax.all_to_all(queries, ("row", "col"), split_axis=1, concat_axis=0, tiled=True),
        lax.all_to_all(out_grad, ("row", "col"), split_axis=1, concat_axis=0, tiled=True),
    )
    kv_range = jnp.arange(KV, dtype=jnp.int32)
    owner = jnp.arange(group_size, dtype=jnp.int32) // sources_each
    chosen = jnp.sum(jnp.where(owner[:, None] == kv_range[None, :], kv_order[None, :], 0), axis=1)
    pick_table = (kv_range[:, None] == chosen[None, :]).astype(jnp.bfloat16)
    key_send = jnp.einsum(
        "tkd,kj->tjd",
        keys.reshape(token_dev, KV, HD),
        pick_table,
        preferred_element_type=jnp.float32,
    ).astype(jnp.bfloat16)
    value_send = jnp.einsum(
        "tkd,kj->tjd",
        values.reshape(token_dev, KV, HD),
        pick_table,
        preferred_element_type=jnp.float32,
    ).astype(jnp.bfloat16)
    key_got, value_got = (
        lax.all_to_all(key_send, ("row", "col"), split_axis=1, concat_axis=0, tiled=True),
        lax.all_to_all(value_send, ("row", "col"), split_axis=1, concat_axis=0, tiled=True),
    )
    key_full = key_got.reshape(length_total, HD)
    value_full = value_got.reshape(length_total, HD)
    parts = token_parts(lengths[0], length_total)
    document = parts // 2
    response = (parts % 2).astype(jnp.bfloat16)
    head_grad = head_grad * response[:, None]
    row_block = min(512, length_total)
    grad_query, grad_key, grad_value = attend_head(
        head_query, key_full, value_full, head_grad, document, row_block, reach
    )
    key_back, value_back = (
        lax.all_to_all(
            grad_key.reshape(group_size, token_dev, HD),
            ("row", "col"),
            split_axis=0,
            concat_axis=0,
            tiled=True,
        ),
        lax.all_to_all(
            grad_value.reshape(group_size, token_dev, HD),
            ("row", "col"),
            split_axis=0,
            concat_axis=0,
            tiled=True,
        ),
    )
    order_table = (kv_order[:, None] == kv_range[None, :]).astype(jnp.float32)

    def place_heads(stacked):
        summed = jnp.sum(stacked.reshape(KV, sources_each, token_dev, HD), axis=1)
        placed = jnp.einsum("mtd,mk->tkd", summed, order_table, precision=lax.Precision.HIGHEST)
        return placed.reshape(token_dev, KV * HD)

    key_grad = place_heads(key_back)
    value_grad = place_heads(value_back)
    arranged = grad_query.reshape(columns_count, rows_count, token_dev, heads_dev * HD)
    arranged = arranged.transpose(1, 0, 2, 3).reshape(length_total, heads_dev * HD)
    shard_query = lax.all_to_all(arranged, ("row", "col"), split_axis=0, concat_axis=1, tiled=True)
    block_query = lax.all_gather(shard_query, "row", axis=0, tiled=True)
    used = block_query
    input_grad = jnp.dot(
        used,
        lax.all_gather(q_weight, "col", axis=0, tiled=True),
        preferred_element_type=jnp.float32,
    ).astype(jnp.bfloat16)
    used = block_query
    weight_grad = lax.psum_scatter(
        lax.dot_general(
            used, hidden_in, (((0,), (0,)), ((), ())), preferred_element_type=jnp.float32
        ),
        ("rollout", "col"),
        scatter_dimension=0,
        tiled=True,
    )
    return (key_grad, value_grad, input_grad, weight_grad)


def solution(mesh):
    placed = (
        P(("rollout", "row", "col"), None),
        P(("rollout", "row", "col"), None),
        P(("rollout", "row", "col"), None),
        P(("rollout", "row", "col"), None),
        P(("rollout", "col"), "row"),
        P("col", "row"),
        P("rollout", None),
        P(),
    )
    return jax.shard_map(
        body,
        mesh=mesh,
        in_specs=placed,
        out_specs=(
            P(("rollout", "row", "col"), None),
            P(("rollout", "row", "col"), None),
            P(("rollout", "col"), "row"),
            P(("rollout", "col"), "row"),
        ),
        check_vma=False,
    )
```

profile of v0, /device:TPU:1, one launch (start us, length us, event | category | flops | bytes accessed | tf_op | source)
XLA Modules:
  0.0 613.1 jit_solution(12362430108168158145)
XLA Ops:
  10.9 11.5 %all-to-all-start = ((bf16[128,32,128]{2,0,1:T(8,128)(2,1)}), bf16[128,32,128]{2,0,1:T(8,128)(2,1)S(1)}, u32[]{:S(2)}, u32[]{:S(2)}) async-start(bf16[128,32,128]{2,0,1:T(8,128)(2,1)} %copy.141), calls=%async_computation | async-start | bytes 2097152 | tf_op jit(solution)/shard_map/all_to_all | solution.py:93
  22.4 2.3 copy.142
  24.7 13.9 %all-to-all-done = bf16[128,32,128]{2,0,1:T(8,128)(2,1)S(1)} async-done(((bf16[128,32,128]{2,0,1:T(8,128)(2,1)}), bf16[128,32,128]{2,0,1:T(8,128)(2,1)S(1)}, u32[]{:S(2)}, u32[]{:S(2)}) %all-to-all-start) | async-done | bytes 1048608 | tf_op jit(solution)/shard_map/all_to_all | solution.py:93
  38.6 6.0 all-to-all-start.1
  44.6 1.5 fusion.15
  46.4 2.6 copy.147
  49.0 2.3 copy.145
  56.5 3.5 all-to-all-done.1
  60.0 6.9 %all-to-all-start.3 = ((bf16[128,32,128]{2,0,1:T(8,128)(2,1)}), bf16[128,32,128]{2,0,1:T(8,128)(2,1)}, u32[]{:S(2)}, u32[]{:S(2)}) async-start(bf16[128,32,128]{2,0,1:T(8,128)(2,1)} %copy.147), calls=%async_computation.3 | async-start | bytes 2097152 | tf_op jit(solution)/shard_map/all_to_all | solution.py:94
  70.1 12.2 %all-to-all-done.3 = bf16[128,32,128]{2,0,1:T(8,128)(2,1)} async-done(((bf16[128,32,128]{2,0,1:T(8,128)(2,1)}), bf16[128,32,128]{2,0,1:T(8,128)(2,1)}, u32[]{:S(2)}, u32[]{:S(2)}) %all-to-all-start.3) | async-done | bytes 1048608 | tf_op jit(solution)/shard_map/all_to_all | solution.py:94
  82.3 6.9 %all-to-all-start.2 = ((bf16[128,32,128]{0,2,1:T(8,128)(2,1)}), bf16[128,32,128]{0,2,1:T(8,128)(2,1)}, u32[]{:S(2)}, u32[]{:S(2)}) async-start(bf16[128,32,128]{0,2,1:T(8,128)(2,1)} %bitcast.153), calls=%async_computation.2 | async-start | bytes 2097152 | tf_op jit(solution)/shard_map/all_to_all | solution.py:74
  90.5 2.3 fusion.100
  92.9 1.6 slice.662
  95.7 2.8 fusion.102
  98.5 6.0 all-to-all-done.2
  104.5 1.6 copy.146
  106.1 1.7 copy.148
  107.8 1.7 copy.151
  109.5 1.7 copy.154
  111.1 1.7 copy.157
  112.8 1.7 copy.160
  114.5 1.7 copy.163
  116.1 1.7 copy.166
  146.6 22.1 %all_to_all.94 = bf16[32,128,128]{2,1,0:T(8,128)(2,1)} all-to-all(bf16[32,128,128]{2,1,0:T(8,128)(2,1)S(1)} %bitcast.156), channel_id=1, replica_groups=mesh['rollout'=4,'row'=8,'col'=4] {'row','col'}, dimensions={0} | all-to-all | bytes 2097152 | tf_op jit(solution)/shard_map/all_to_all | solution.py:133
  168.6 2.3 copy.172
  171.7 118.2 %all-gather.3.cloned.1.call-done = bf16[1024,4096]{0,1:T(8,128)(2,1)} async-done(((bf16[128,4096]{0,1:T(8,128)(2,1)}), bf16[1024,4096]{0,1:T(8,128)(2,1)}) %all-gather.3.cloned.1.call-update) | async-done | bytes 8388624 | tf_op jit(solution)/shard_map/all_gather | solution.py:134
  289.9 15.2 %fusion.114 = f32[4096,1024]{1,0:T(8,128)} fusion(bf16[1024,4096]{0,1:T(8,128)(2,1)} %all-gather.3.cloned.1.call-done, bf16[1024,1024]{1,0:T(8,128)(2,1)S(1)} %copy-done), kind=kOutput, calls=%fused_computation.197 | convolution fusion | flops 8589934592 | bytes 27262976 | tf_op jit(solution)/shard_map/dot_general | solution.py:143
  306.6 1.5 scatter-add.54
  309.3 2.4 fusion.30
  311.6 2.4 fusion.29
  314.0 2.4 fusion.28
  316.4 2.4 fusion.27
  318.8 2.3 fusion.26
  321.1 2.3 fusion.25
  323.4 6.6 %all-to-all-start.4 = ((f32[32,128,128]{2,1,0:T(8,128)}), f32[32,128,128]{2,1,0:T(8,128)S(1)}, u32[]{:S(2)}, u32[]{:S(2)}) async-start(f32[32,128,128]{2,1,0:T(8,128)} %bitcast.48), calls=%async_computation.4 | async-start | bytes 4194304 | tf_op jit(solution)/shard_map/all_to_all | solution.py:107
  335.5 2.5 fusion.23
  338.0 2.5 fusion.22
  340.6 2.5 fusion.21
  343.1 2.5 fusion.20
  345.6 2.5 fusion.19
  348.1 2.4 fusion.18
  350.4 6.6 %all-to-all-done.4 = f32[32,128,128]{2,1,0:T(8,128)S(1)} async-done(((f32[32,128,128]{2,1,0:T(8,128)}), f32[32,128,128]{2,1,0:T(8,128)S(1)}, u32[]{:S(2)}, u32[]{:S(2)}) %all-to-all-start.4) | async-done | bytes 2097184 | tf_op jit(solution)/shard_map/all_to_all | solution.py:107
  357.0 10.1 %all-to-all-start.5 = ((f32[32,128,128]{2,1,0:T(8,128)}), f32[32,128,128]{2,1,0:T(8,128)}, u32[]{:S(2)}, u32[]{:S(2)}) async-start(f32[32,128,128]{2,1,0:T(8,128)} %bitcast.51), calls=%async_computation.5 | async-start | bytes 4194304 | tf_op jit(solution)/shard_map/all_to_all | solution.py:114
  369.0 26.8 %all-to-all-done.5 = f32[32,128,128]{2,1,0:T(8,128)} async-done(((f32[32,128,128]{2,1,0:T(8,128)}), f32[32,128,128]{2,1,0:T(8,128)}, u32[]{:S(2)}, u32[]{:S(2)}) %all-to-all-start.5) | async-done | bytes 2097184 | tf_op jit(solution)/shard_map/all_to_all | solution.py:114
  395.8 1.7 bitcast_reduce_fusion
  398.8 21.5 %all-gather.5.cloned.1.call-done = bf16[4096,1024]{1,0:T(8,128)(2,1)} async-done(((bf16[1024,1024]{1,0:T(8,128)(2,1)}), bf16[4096,1024]{1,0:T(8,128)(2,1)}) %all-gather.5.cloned.1.call-update) | async-done | bytes 8388624 | tf_op jit(solution)/shard_map/all_gather | solution.py:138
  420.3 14.8 %convolution_convert_fusion = bf16[1024,1024]{1,0:T(8,128)(2,1)} fusion(bf16[1024,4096]{0,1:T(8,128)(2,1)} %all-gather.3.cloned.1.call-done, bf16[4096,1024]{1,0:T(8,128)(2,1)} %all-gather.5.cloned.1.call-done), kind=kOutput, calls=%fused_computation.30 | convolution fusion | flops 8590983168 | bytes 18874368 | tf_op jit(solution)/shard_map/dot_general | solution.py:136
  435.1 171.2 %reduce-scatter.2.cloned.1.call-done = f32[256,1024]{1,0:T(8,128)} async-done(((f32[4096,1024]{1,0:T(8,128)}), f32[256,1024]{1,0:T(8,128)}) %reduce-scatter.2.cloned.1.call-update) | async-done | bytes 1048592 | tf_op jit(solution)/shard_map/reduce_scatter | solution.py:142
  (323 shorter events, 55.2 us)
Async XLA Ops:
  7.2 282.7 %copy-start = (bf16[1024,1024]{1,0:T(8,128)(2,1)S(1)}, bf16[1024,1024]{1,0:T(8,128)(2,1)}, u32[]{:S(2)}) copy-start(bf16[1024,1024]{1,0:T(8,128)(2,1)} %param.44) | copy-start | bytes 6291460
  10.9 13.8 %copy-start.62 = (bf16[128,512]{1,0:T(8,128)(2,1)S(1)}, bf16[128,512]{1,0:T(8,128)(2,1)}, u32[]{:S(2)}) copy-start(bf16[128,512]{1,0:T(8,128)(2,1)} %param.42) | copy-start | bytes 393220
  10.9 27.7 %all-to-all-start = ((bf16[128,32,128]{2,0,1:T(8,128)(2,1)}), bf16[128,32,128]{2,0,1:T(8,128)(2,1)S(1)}, u32[]{:S(2)}, u32[]{:S(2)}) async-start(bf16[128,32,128]{2,0,1:T(8,128)(2,1)} %copy.141), calls=%async_computation | async-start | bytes 2097152 | tf_op jit(solution)/shard_map/all_to_all | solution.py:93
  24.7 21.5 %copy-start.117 = (s32[1,32]{1,0:T(1,128)S(1)}, s32[1,32]{1,0:T(1,128)}, u32[]{:S(2)}) copy-start(s32[1,32]{1,0:T(1,128)} %param.46) | copy-start | bytes 388
  38.6 21.4 %all-to-all-start.1 = ((bf16[128,32,128]{0,2,1:T(8,128)(2,1)}), bf16[128,32,128]{0,2,1:T(8,128)(2,1)}, u32[]{:S(2)}, u32[]{:S(2)}) async-start(bf16[128,32,128]{0,2,1:T(8,128)(2,1)} %bitcast.154), calls=%async_computation.1 | async-start | bytes 2097152 | tf_op jit(solution)/shard_map/all_to_all | solution.py:73
  60.0 22.2 %all-to-all-start.3 = ((bf16[128,32,128]{2,0,1:T(8,128)(2,1)}), bf16[128,32,128]{2,0,1:T(8,128)(2,1)}, u32[]{:S(2)}, u32[]{:S(2)}) async-start(bf16[128,32,128]{2,0,1:T(8,128)(2,1)} %copy.147), calls=%async_computation.3 | async-start | bytes 2097152 | tf_op jit(solution)/shard_map/all_to_all | solution.py:94
  82.3 22.2 %all-to-all-start.2 = ((bf16[128,32,128]{0,2,1:T(8,128)(2,1)}), bf16[128,32,128]{0,2,1:T(8,128)(2,1)}, u32[]{:S(2)}, u32[]{:S(2)}) async-start(bf16[128,32,128]{0,2,1:T(8,128)(2,1)} %bitcast.153), calls=%async_computation.2 | async-start | bytes 2097152 | tf_op jit(solution)/shard_map/all_to_all | solution.py:74
  89.1 200.8 %all-gather.3.cloned.1.call-start = ((), (), s32[]{:S(2)}) async-start(), calls=%async_computation.8 | async-start | bytes 9437184 | tf_op jit(solution)/shard_map/all_gather | solution.py:134
  117.8 2.9 copy-start.63
  120.6 20.5 %copy-start.38 = (bf16[4096,128]{1,0:T(8,128)(2,1)}, bf16[4096,128]{1,0:T(8,128)(2,1)S(1)}, u32[]{:S(2)}) copy-start(bf16[4096,128]{1,0:T(8,128)(2,1)S(1)} %bitcast_multiply_fusion) | copy-start | bytes 3145732
  127.9 15.3 %copy-start.2 = (bf16[512,1024]{0,1:T(8,128)(2,1)}, bf16[512,1024]{0,1:T(8,128)(2,1)S(1)}, u32[]{:S(2)}) copy-start(bf16[512,1024]{0,1:T(8,128)(2,1)S(1)} %multiply_convert_fusion.5) | copy-start | bytes 3145732
  130.8 13.0 %copy-start.4 = (bf16[512,1024]{0,1:T(8,128)(2,1)}, bf16[512,1024]{0,1:T(8,128)(2,1)S(1)}, u32[]{:S(2)}) copy-start(bf16[512,1024]{0,1:T(8,128)(2,1)S(1)} %multiply_convert_fusion.4) | copy-start | bytes 3145732
  133.8 10.5 %copy-start.6 = (bf16[512,1024]{0,1:T(8,128)(2,1)}, bf16[512,1024]{0,1:T(8,128)(2,1)S(1)}, u32[]{:S(2)}) copy-start(bf16[512,1024]{0,1:T(8,128)(2,1)S(1)} %multiply_convert_fusion.3) | copy-start | bytes 3145732
  136.7 8.1 %copy-start.8 = (bf16[512,1024]{0,1:T(8,128)(2,1)}, bf16[512,1024]{0,1:T(8,128)(2,1)S(1)}, u32[]{:S(2)}) copy-start(bf16[512,1024]{0,1:T(8,128)(2,1)S(1)} %multiply_convert_fusion.2) | copy-start | bytes 3145732
  139.9 5.6 copy-start.10
  142.7 3.3 copy-start.12
  170.9 249.3 %all-gather.5.cloned.1.call-start = ((), (), s32[]{:S(2)}) async-start(), calls=%async_computation.9 | async-start | bytes 10485760 | tf_op jit(solution)/shard_map/all_gather | solution.py:138
  171.7 434.6 %reduce-scatter.2.cloned.1.call-start = ((), (), s32[]{:S(2)}) async-start(), calls=%async_computation.10 | async-start | bytes 17825792 | tf_op jit(solution)/shard_map/reduce_scatter | solution.py:142
  306.5 2.7 copy-start.3
  306.5 2.7 copy-start.51
  308.0 3.6 copy-start.5
  308.0 3.6 copy-start.49
  309.2 4.8 copy-start.7
  309.3 4.8 copy-start.47
  311.6 4.8 copy-start.9
  311.6 4.8 copy-start.45
  314.0 4.8 copy-start.11
  314.0 4.8 copy-start.43
  316.4 4.7 copy-start.13
  316.4 4.7 copy-start.41
  323.3 6.6 %copy-start.31 = (f32[512,512]{0,1:T(8,128)S(1)}, f32[512,512]{0,1:T(8,128)}, u32[]{:S(2)}) copy-start(f32[512,512]{0,1:T(8,128)} %copy-done.30) | copy-start | bytes 3145732
  323.4 33.7 %all-to-all-start.4 = ((f32[32,128,128]{2,1,0:T(8,128)}), f32[32,128,128]{2,1,0:T(8,128)S(1)}, u32[]{:S(2)}, u32[]{:S(2)}) async-start(f32[32,128,128]{2,1,0:T(8,128)} %bitcast.48), calls=%async_computation.4 | async-start | bytes 4194304 | tf_op jit(solution)/shard_map/all_to_all | solution.py:107
  329.9 2.8 copy-start.39
  335.4 2.6 copy-start.19
  335.4 2.6 copy-start.69
  335.4 2.6 copy-start.71
  338.0 2.5 copy-start.21
  338.0 2.5 copy-start.73
  338.0 2.5 copy-start.75
  340.5 2.5 copy-start.23
  340.5 2.5 copy-start.77
  340.5 2.5 copy-start.79
  343.0 2.5 copy-start.25
  343.0 2.5 copy-start.81
  343.1 2.5 copy-start.83
  345.6 2.5 copy-start.27
  357.0 38.8 %all-to-all-start.5 = ((f32[32,128,128]{2,1,0:T(8,128)}), f32[32,128,128]{2,1,0:T(8,128)}, u32[]{:S(2)}, u32[]{:S(2)}) async-start(f32[32,128,128]{2,1,0:T(8,128)} %bitcast.51), calls=%async_computation.5 | async-start | bytes 4194304 | tf_op jit(solution)/shard_map/all_to_all | solution.py:114
  420.3 186.0 %copy-start.1 = (bf16[1024,1024]{1,0:T(8,128)(2,1)S(1)}, bf16[1024,1024]{1,0:T(8,128)(2,1)}, u32[]{:S(2)}) copy-start(bf16[1024,1024]{1,0:T(8,128)(2,1)} %param.44) | copy-start | bytes 6291460
  (79 other events, 91.6 us)
Sparse Core Ops, SparseCore 0:
  171.1 118.8 all-gather.2
  291.6 128.6 all-gather.4
  423.2 182.9 reduce-scatter.1
where the time goes:
time: 620 us; the launch traced here: 613 us
  waiting for transfers between devices  381 us (61%)
  matrix products  79.8 us (13%)
  starting transfers between devices  48 us (8%)
  local copies, waits for them, and re-layouts  47.1 us (8%)
  blocking collectives  22.1 us (4%)
  other arithmetic  20.2 us (3%)
  between operations  15.2 us (2%)
    reduce_scatter x1, waiting for transfers between devices, body(): lax.psum_scatter(lax.dot_general(used, hidden_in, (((0,), (0,)), ((), ())...  171 us
    all_gather x1, waiting for transfers between devices, body(): block_query = lax.all_gather(shard_query, 'row', axis=0, tiled=True)  118 us
    all_to_all x1, waiting for transfers between devices, body(): lax.all_to_all(grad_value.reshape(group_size, token_dev, HD), ('row', 'co...  26.8 us
    all_to_all x1, blocking collectives, body(): lax.all_to_all(arranged, ('row', 'col'), split_axis=0, concat_axis=1, til...  22.1 us
    all_gather x1, waiting for transfers between devices, body(): lax.all_gather(q_weight, 'col', axis=0, tiled=True)  21.5 us
    dot_general x8, matrix products, attend_head(): jnp.einsum('qk,qd->kd', attention_half, grad_rows, preferred_element_type...  17.4 us
    dot_general x8, matrix products, attend_head(): jnp.einsum('qk,qd->kd', grad_scores, query_rows, preferred_element_type=j...  15.5 us
    dot_general x1, matrix products, body(): lax.dot_general(used, hidden_in, (((0,), (0,)), ((), ())), preferred_elem...  15.2 us
  transfers between devices with their start and end apart: 9, of which 9 were waited for; matrix products, arithmetic and copies ran while one was open for 16% of the time, Pallas kernels for 0%

commit v1 on v0

v1 whole, which is shorter than its diff:
```python
import functools
import math

import jax
import jax.numpy as jnp
from jax import lax
from jax.experimental import pallas as pl
from jax.experimental.pallas import tpu as pltpu
from jax.sharding import PartitionSpec as P

HQ = 32
KV = 4
HD = 128
ROLLS = 16
BF = jnp.bfloat16
F32 = jnp.float32
SCALE = 1.0 / math.sqrt(HD)
SCALE2 = SCALE * math.log2(math.e)
NEG = -1e30
BACK = 4
TB = 128

NT = (((1,), (1,)), ((), ()))
NN = (((1,), (0,)), ((), ()))


def dot(a, b, dims=NN):
    return lax.dot_general(a, b, dims, preferred_element_type=F32)


def attend_kernel(parity, first, order_ref, block_ref, core_ref, len_ref, *refs):
    q_refs, g_refs = refs[0:4], refs[4:8]
    k_refs, v_refs = refs[8:13], refs[13:18]
    rest = refs[18:]
    if first:
        acc_in = None
        qg_ref, acc_out = rest[0:2]
        bias_ref, resp_ref = rest[2:4]
    else:
        acc_in = rest[0]
        qg_ref, own_ref = rest[1:3]
        back_refs = rest[3:7]
        bias_ref, resp_ref = rest[7:9]
    j = pl.program_id(0)

    @pl.when(j == 0)
    def _():
        base = block_ref[0] * TB
        query_pos = base + lax.broadcasted_iota(jnp.int32, (8, TB), 1)
        start = jnp.zeros((8, TB), jnp.int32)
        part = jnp.zeros((8, TB), jnp.int32)
        bound = jnp.int32(0)
        for k in range(2 * ROLLS):
            bound = bound + len_ref[k]
            passed = query_pos >= bound
            part = part + passed.astype(jnp.int32)
            if k % 2 == 1:
                start = jnp.where(passed, bound, start)
        resp_ref[...] = (part % 2).astype(F32)
        key_pos = base - BACK * TB + lax.broadcasted_iota(jnp.int32, ((BACK + 1) * TB, TB), 0)
        allowed = (key_pos >= start[0:1]) & (key_pos <= query_pos[0:1])
        bias_ref[...] = jnp.where(allowed, 0.0, NEG)

    keys = jnp.concatenate([r[...] for r in k_refs], axis=0)
    vals = jnp.concatenate([r[...] for r in v_refs], axis=0)
    keys_t = keys.T
    bias = bias_ref[...]
    bias = jnp.concatenate([bias, bias], axis=1)
    resp = resp_ref[0:1, :]
    resp = jnp.concatenate([resp, resp], axis=1)
    if first:
        dk = jnp.zeros(((BACK + 1) * TB, HD), F32)
        dv = dk
    else:
        dk = acc_in[0]
        dv = acc_in[1]
    column = ((j + core_ref[0]) % 2) * 8 + (j // 2) * 4
    for pair in range(2):
        query = jnp.concatenate([q_refs[2 * pair][...], q_refs[2 * pair + 1][...]], axis=0)
        grad = jnp.concatenate([g_refs[2 * pair][...], g_refs[2 * pair + 1][...]], axis=0)
        scores = dot(keys, query, NT) + bias
        dprobs = dot(vals, grad, NT)
        top = jnp.max(scores, axis=0, keepdims=True)
        raw = jnp.exp2((scores - top) * SCALE2)
        total = jnp.sum(raw, axis=0, keepdims=True)
        norm = resp / total
        probs = raw * norm
        delta = jnp.sum(probs * dprobs, axis=0, keepdims=True)
        dscores = (raw * (norm * SCALE) * (dprobs - delta)).astype(BF)
        dv = dv + dot(probs.astype(BF), grad)
        dk = dk + dot(dscores, query)
        dq = dot(keys_t, dscores).T.astype(BF)
        for c in range(2):
            at = pl.multiple_of((column + 2 * pair + c) * HD, HD)
            qg_ref[:, pl.ds(at, HD)] = dq[c * TB : (c + 1) * TB]

    if first:
        acc_out[0] = dk
        acc_out[1] = dv
    else:
        for b in range(BACK):
            back_refs[b][0] = dk[b * TB : (b + 1) * TB].astype(BF)
            back_refs[b][1] = dv[b * TB : (b + 1) * TB].astype(BF)
        own_ref[0] = dk[BACK * TB :]
        own_ref[1] = dv[BACK * TB :]


def attend(parity, queries, grads, kv_blocks, order, block, core, lengths, acc):
    first = acc is None

    def head_spec(c):
        return pl.BlockSpec((TB, HD), lambda j, o, *_: (0, 8 * j + 2 * c + parity))

    k_spec = pl.BlockSpec((TB, HD), lambda j, o, *_: (0, o[j]))
    v_spec = pl.BlockSpec((TB, HD), lambda j, o, *_: (0, KV + o[j]))
    wide = (BACK + 1) * TB
    acc_spec = pl.BlockSpec((2, wide, HD), lambda j, o, *_: (0, 0, j))
    qg_spec = pl.BlockSpec((TB, 16 * HD), lambda j, o, *_: (0, 0))
    qg_shape = jax.ShapeDtypeStruct((TB, 16 * HD), BF)
    kv_out = pl.BlockSpec((2, TB, HD), lambda j, o, *_: (0, 0, o[j]))
    in_specs = [head_spec(c) for c in range(4)] * 2 + [k_spec] * 5 + [v_spec] * 5
    args = [queries] * 4 + [grads] * 4 + list(kv_blocks) * 2
    if first:
        out_specs = [qg_spec, acc_spec]
        out_shape = [qg_shape, jax.ShapeDtypeStruct((2, wide, KV * HD), F32)]
    else:
        in_specs = in_specs + [acc_spec]
        args = args + [acc]
        out_specs = [qg_spec] + [kv_out] * (1 + BACK)
        out_shape = (
            [qg_shape]
            + [jax.ShapeDtypeStruct((2, TB, KV * HD), F32)]
            + [jax.ShapeDtypeStruct((2, TB, KV * HD), BF)] * BACK
        )
    return pl.pallas_call(
        functools.partial(attend_kernel, parity, first),
        grid_spec=pltpu.PrefetchScalarGridSpec(
            num_scalar_prefetch=4,
            grid=(KV,),
            in_specs=in_specs,
            out_specs=out_specs,
            scratch_shapes=[pltpu.VMEM((wide, TB), F32), pltpu.VMEM((8, TB), F32)],
        ),
        out_shape=out_shape,
        compiler_params=pltpu.CompilerParams(vmem_limit_bytes=48 << 20),
        cost_estimate=pl.CostEstimate(
            flops=16 * 5 * 2 * wide * TB * HD,
            bytes_accessed=8 << 20,
            transcendentals=16 * wide * TB,
        ),
        name="attend%d" % parity,
    )(order, block, core, lengths, *args)


def reorder_kernel(idx_ref, x_ref, o_ref):
    o_ref[...] = x_ref[...]


def reorder(x, idx):
    n = x.shape[0] // TB
    spec = (TB, x.shape[1])
    return pl.pallas_call(
        reorder_kernel,
        grid_spec=pltpu.PrefetchScalarGridSpec(
            num_scalar_prefetch=1,
            grid=(n,),
            in_specs=[pl.BlockSpec(spec, lambda i, t: (t[i], 0))],
            out_specs=pl.BlockSpec(spec, lambda i, t: (i, 0)),
        ),
        out_shape=jax.ShapeDtypeStruct(x.shape, x.dtype),
        cost_estimate=pl.CostEstimate(flops=0, bytes_accessed=4 << 20, transcendentals=0),
        name="reorder",
    )(idx, x)


def project_kernel(core_ref, arrival_ref, ua_ref, ub_ref, own_ref, other_ref, o_ref, acc_ref):
    step = pl.program_id(0)

    def add(first, second):
        for m in range(4):
            rows = pl.ds(m * 2 * TB, 2 * TB)
            term = dot(ua_ref[rows, :], first[...]) + dot(ub_ref[rows, :], second[...])

            @pl.when(step == 0)
            def _():
                acc_ref[rows, :] = term

            @pl.when(step > 0)
            def _():
                acc_ref[rows, :] += term

    @pl.when(core_ref[0] == 0)
    def _():
        add(own_ref, other_ref)

    @pl.when(core_ref[0] == 1)
    def _():
        add(other_ref, own_ref)

    @pl.when(step == pl.num_programs(0) - 1)
    def _():
        for i in range(acc_ref.shape[0] // TB):
            at = pl.multiple_of(arrival_ref[i] * TB, TB)
            o_ref[pl.ds(at, TB), :] = acc_ref[pl.ds(i * TB, TB), :].astype(BF)


def project(used_a, used_b, w_own, w_other, core, arrival):
    tokens, wide = used_a.shape[0], w_own.shape[1]
    used_spec = pl.BlockSpec((tokens, 4 * TB), lambda i, *_: (0, i))
    w_spec = pl.BlockSpec((4 * TB, wide), lambda i, core, _: (2 * (i % 2) + (core[0] + i // 2) % 2, 0))
    return pl.pallas_call(
        project_kernel,
        grid_spec=pltpu.PrefetchScalarGridSpec(
            num_scalar_prefetch=2,
            grid=(4,),
            in_specs=[used_spec] * 2 + [w_spec] * 2,
            out_specs=pl.BlockSpec((tokens, wide), lambda i, *_: (0, 0)),
            scratch_shapes=[pltpu.VMEM((tokens, wide), F32)],
        ),
        out_shape=jax.ShapeDtypeStruct((tokens, wide), BF),
        compiler_params=pltpu.CompilerParams(vmem_limit_bytes=40 << 20),
        cost_estimate=pl.CostEstimate(
            flops=2 * tokens * wide * 4096, bytes_accessed=18 << 20, transcendentals=0
        ),
        name="project",
    )(core, arrival, used_a, used_b, w_own, w_other)


ROWCOL = ("row", "col")
X_UP = [(r, (r + 2) % 8) for r in range(8)]
X_DOWN = [(r, (r - 2) % 8) for r in range(8)]
Y_SWAP = [(r, r ^ 1) for r in range(8)]
CORE_SWAP = [(r, r ^ 1) for r in range(4)]
ONE_CORE = [[4 * (2 * n + core) + c for n in range(2) for c in range(4)] for core in range(2)]


def shift(n):
    return [(b, b + n) for b in range(32) if 0 <= b + n < 32]


def turn():
    pairs = []
    for x in range(4):
        for y in range(2):
            for z in range(4):
                pairs.append(((2 * x + y) * 4 + z, (2 * ((x + z) % 4) + y) * 4 + x))
    return pairs


TURN = turn()


def tie(x, *others):
    return lax.optimization_barrier((x, *others))[0]


def up(x):
    return lax.ppermute(x, "row", X_UP)


def down(x):
    return lax.ppermute(x, "row", X_DOWN)


def swap_y(x):
    return lax.ppermute(x, "row", Y_SWAP)


def share(t0):
    h = TB // 2
    t1 = up(t0)
    t3 = down(t0)
    y0 = swap_y(t0)
    t2 = jnp.concatenate([up(t1[:h]), down(t3[h:])], axis=0)
    y1 = up(y0)
    y3 = down(y0)

    def rest(*after):
        y2 = swap_y(tie(t2, *after))
        return jnp.concatenate([t0, t3, t2, t1, y0, y3, y2, y1], axis=0)

    return rest


def body(queries, keys, values, out_grad, hidden_in, q_weight, lengths, kv_order):
    row = lax.axis_index("row")
    col = lax.axis_index("col")
    rollout = lax.axis_index("rollout")
    core = rollout % 2
    x, y = row // 2, row % 2
    block = (row * 4 + col).astype(jnp.int32).reshape(1)
    core1 = core.astype(jnp.int32).reshape(1)
    wide = q_weight.shape[1]

    kv = jnp.concatenate([keys, values], axis=1)
    kv_blocks = [lax.ppermute(kv, ROWCOL, shift(n)) for n in (4, 3, 2, 1)] + [kv]

    k = (x - col) % 4
    arrival = jnp.stack(
        [4 * (y ^ s) + (k + n) % 4 for s in range(2) for n in range(4)]
    ).astype(jnp.int32)
    hidden = reorder(hidden_in, arrival)
    block = tie(block, hidden)

    lens = lengths[0]
    qa, acc = attend(0, queries, out_grad, kv_blocks, kv_order, block, core1, lens, None)
    outs = attend(1, queries, out_grad, kv_blocks, kv_order, block, core1, lens, acc)
    qb, own = outs[:2]
    back = outs[2:]

    dims = (((0,), (0,)), ((), ()))

    def send_part(used):
        return dot(used[:, used.shape[1] // 2 :], hidden, dims).astype(BF)

    def lower(used, send):
        half = used.shape[1] // 2
        came = lax.ppermute(send, "rollout", CORE_SWAP)
        return (dot(used[:, :half], hidden, dims) + came.astype(F32)).astype(BF)

    def collect(low):
        return lax.all_to_all(
            low, ("rollout", "col"), 0, 0, axis_index_groups=ONE_CORE, tiled=True
        )

    def sum_rows(got):
        return jnp.sum(got.reshape(8, TB, wide).astype(F32), axis=0)

    turn_a = lax.ppermute(qa, ROWCOL, TURN)
    turn_b = lax.ppermute(tie(qb, turn_a), ROWCOL, TURN)

    mine = lax.dynamic_index_in_dim(q_weight.reshape(4, 2, TB, wide), core, 1, keepdims=False)
    mine = tie(mine.reshape(4 * TB, wide), turn_b)
    w_own = lax.all_gather(mine, "col", axis=0, tiled=True)

    rest_a = share(turn_a)
    rest_b = share(turn_b)
    used_a = rest_a()
    send_a = send_part(used_a)
    low_a = lower(used_a, send_a)
    back = [tie(b, turn_a) for b in back]
    total = own
    for b in range(BACK):
        total = total + lax.ppermute(back[b], ROWCOL, shift(b - BACK)).astype(F32)
    used_b = rest_b(low_a, total)
    got_a = collect(low_a)
    w_own = tie(w_own, used_b)
    w_other = lax.ppermute(w_own, "rollout", CORE_SWAP)
    send_b = send_part(used_b)
    low_b = lower(used_b, send_b)
    got_b = collect(low_b)
    input_grad = project(used_a, used_b, w_own, w_other, core1, arrival)
    got_b = tie(got_b, input_grad)
    weight_grad = jnp.concatenate([sum_rows(got_a), sum_rows(got_b)], axis=0)
    return (total[0], total[1], input_grad, weight_grad)


def solution(mesh):
    placed = (
        P(("rollout", "row", "col"), None),
        P(("rollout", "row", "col"), None),
        P(("rollout", "row", "col"), None),
        P(("rollout", "row", "col"), None),
        P(("rollout", "col"), "row"),
        P("col", "row"),
        P("rollout", None),
        P(),
    )
    return jax.shard_map(
        body,
        mesh=mesh,
        in_specs=placed,
        out_specs=(
            P(("rollout", "row", "col"), None),
            P(("rollout", "row", "col"), None),
            P(("rollout", "col"), "row"),
            P(("rollout", "col"), "row"),
        ),
        check_vma=False,
    )
```

time: 620 us -> 281 us (0.45)
  waiting for transfers between devices: 381 us -> 54.6 us
  matrix products: 79.8 us -> 20.7 us
  starting transfers between devices: 48 us -> 104 us
  Pallas kernels: 0 us -> 45.4 us
  blocking collectives: 22.1 us -> 0 us
  other arithmetic: 20.2 us -> 5.35 us
  local copies, waits for them, and re-layouts: 47.1 us -> 35.3 us
    reduce_scatter x1 -> x0, waiting for transfers between devices: 171 us -> none  [body(): lax.psum_scatter(lax.dot_general(used, hidden_in, (((0,), (0,)), ((), ())...]
    all_gather x2 -> x1, waiting for transfers between devices: 140 us -> 0.01 us  [body(): w_own = lax.all_gather(mine, 'col', axis=0, tiled=True)]
    ppermute x0 -> x29, starting transfers between devices: none -> 95.5 us  [the longest x6 30.2 us: up(): return lax.ppermute(x, 'row', X_UP)]
    dot_general x46 -> x4, matrix products: 79.8 us -> 20.7 us  [dot(): return lax.dot_general(a, b, dims, preferred_element_type=F32)]
    all_to_all x6 -> x2, waiting for transfers between devices: 69.1 us -> 21.4 us  [collect(): lax.all_to_all(low, ('rollout', 'col'), 0, 0, axis_index_groups=ONE_CORE,...]
    pallas_call x0 -> x4, Pallas kernels: none -> 45.4 us  [the longest x2 22.3 us: attend(): pl.pallas_call(functools.partial(attend_kernel, parity, first), grid_spec...]
    all_to_all x6 -> x2, starting transfers between devices: 47.9 us -> 8.92 us  [collect(): lax.all_to_all(low, ('rollout', 'col'), 0, 0, axis_index_groups=ONE_CORE,...]
    ppermute x0 -> x29, waiting for transfers between devices: none -> 33.2 us  [the longest x4 12.3 us: body(): total = total + lax.ppermute(back[b], ROWCOL, shift(b - BACK)).astype(F32)]
  transfers between devices with their start and end apart: 9 -> 32, of which waited for: 9 -> 11; matrix products, arithmetic and copies ran while one was open for 16% -> 17% of each run, Pallas kernels for 0% -> 13%
where the time goes in v1:
time: 281 us; the launch traced here: 280 us
  starting transfers between devices  104 us (37%)
  waiting for transfers between devices  54.6 us (19%)
  Pallas kernels  45.4 us (16%)
  local copies, waits for them, and re-layouts  35.3 us (13%)
  matrix products  20.7 us (7%)
  between operations  14.4 us (5%)
  other arithmetic  5.35 us (2%)
    ppermute x6, starting transfers between devices, up(): return lax.ppermute(x, 'row', X_UP)  30.2 us
    unnamed x57, local copies, waits for them, and re-layouts  27.4 us
    ppermute x6, starting transfers between devices, down(): return lax.ppermute(x, 'row', X_DOWN)  23.3 us
    pallas_call x2, Pallas kernels, attend(): pl.pallas_call(functools.partial(attend_kernel, parity, first), grid_spec...  22.3 us
    all_to_all x2, waiting for transfers between devices, collect(): lax.all_to_all(low, ('rollout', 'col'), 0, 0, axis_index_groups=ONE_CORE,...  21.4 us
    dot_general x4, matrix products, dot(): return lax.dot_general(a, b, dims, preferred_element_type=F32)  20.7 us
    ppermute x4, starting transfers between devices, body(): lax.ppermute(kv, ROWCOL, shift(n))  17.9 us
    pallas_call x1, Pallas kernels, project(): pl.pallas_call(project_kernel, grid_spec=pltpu.PrefetchScalarGridSpec(num...  16.8 us
  transfers between devices with their start and end apart: 32, of which 11 were waited for; matrix products, arithmetic and copies ran while one was open for 17% of the time, Pallas kernels for 13%

profile of v1, /device:TPU:1, one launch (start us, length us, event | category | flops | bytes accessed | tf_op | source)
XLA Modules:
  0.0 280.2 jit_solution(8622214680529979385)
XLA Ops:
  9.2 6.3 %collective-permute-start = (bf16[128,1024]{1,0:T(8,128)(2,1)S(1)}, bf16[128,1024]{1,0:T(8,128)(2,1)}, u32[]{:S(2)}, u32[]{:S(2)}) collective-permute-start(bf16[128,1024]{1,0:T(8,128)(2,1)S(1)} %constant_dynamic-update-slice_fusion.refs_12_.refs_17_), channel_id=1, source_target_pairs={{0,4},{1,5},{2,6},{3,7},{4,8},{5,9},{6,10},{7,11},{8,12},{9,13},{1... | collective-permute-start | bytes 786440 | tf_op jit(solution)/shard_map/ppermute | solution.py:296
  15.6 6.3 %collective-permute-start.1 = (bf16[128,1024]{1,0:T(8,128)(2,1)S(1)}, bf16[128,1024]{1,0:T(8,128)(2,1)}, u32[]{:S(2)}, u32[]{:S(2)}) collective-permute-start(bf16[128,1024]{1,0:T(8,128)(2,1)S(1)} %constant_dynamic-update-slice_fusion.refs_12_.refs_17_), channel_id=1, source_target_pairs={{0,3},{1,4},{2,5},{3,6},{4,7},{5,8},{6,9},{7,10},{8,11},{9,12},{10... | collective-permute-start | bytes 786440 | tf_op jit(solution)/shard_map/ppermute | solution.py:296
  21.9 2.3 collective-permute-start.2
  24.2 3.0 %collective-permute-start.3 = (bf16[128,1024]{1,0:T(8,128)(2,1)S(1)}, bf16[128,1024]{1,0:T(8,128)(2,1)}, u32[]{:S(2)}, u32[]{:S(2)}) collective-permute-start(bf16[128,1024]{1,0:T(8,128)(2,1)S(1)} %constant_dynamic-update-slice_fusion.refs_12_.refs_17_), channel_id=1, source_target_pairs={{0,1},{1,2},{2,3},{3,4},{4,5},{5,6},{6,7},{7,8},{8,9},{9,10},{10,1... | collective-permute-start | bytes 786440 | tf_op jit(solution)/shard_map/ppermute | solution.py:296
  27.8 6.3 %reorder.1 = bf16[1024,1024]{1,0:T(8,128)(2,1)} custom-call(s32[8]{0:T(128)} %stack.35.idx_ref.arrival_ref, bf16[1024,1024]{1,0:T(8,128)(2,1)} %x_ref.1), custom_call_target="tpu_custom_call" | custom-call | bytes 4194304 | tf_op jit(solution)/shard_map/reorder/pallas_call | solution.py:162
  35.4 10.3 %attend0.1 = (bf16[128,2048]{1,0:T(8,128)(2,1)S(1)}, f32[2,640,512]{2,1,0:T(8,128)}) custom-call(s32[4]{0:T(128)S(1)} %copy-done.7, s32[1]{0:T(128)} %bitcast.block_ref, s32[1]{0:T(128)} %bitcast.9.core_ref, s32[32]{0:T(128)S(1)} %bitcast.29, bf16[128,4096]{1,0:T(8,128)(2,1)S(1)} %copy-done.1, bf16[128,4096]{1,0:T(8,128)(2,1)S(1)} %copy-done.1, ...), custom_call_target="tpu_custom_call" | custom-call | flops 1677721600 | bytes 8388608 | tf_op jit(solution)/shard_map/attend0/pallas_call | solution.py:135
  45.7 1.4 collective-permute-start.4
  47.2 22.9 %collective-permute-start.10 = (bf16[128,2048]{1,0:T(8,128)(2,1)}, bf16[128,2048]{1,0:T(8,128)(2,1)}, u32[]{:S(2)}, u32[]{:S(2)}) collective-permute-start(bf16[128,2048]{1,0:T(8,128)(2,1)} %collective-permute-done.4), channel_id=1, source_target_pairs={{0,8},{4,12},{8,16},{12,20},{16,24},{20,28},{24,0},{28,4},{1,9},{5... | collective-permute-start | bytes 1572872 | tf_op jit(solution)/shard_map/ppermute | solution.py:258
  70.0 3.7 %collective-permute-start.9 = (bf16[128,2048]{1,0:T(8,128)(2,1)}, bf16[128,2048]{1,0:T(8,128)(2,1)}, u32[]{:S(2)}, u32[]{:S(2)}) collective-permute-start(bf16[128,2048]{1,0:T(8,128)(2,1)} %collective-permute-done.4), channel_id=1, source_target_pairs={{0,24},{4,28},{8,0},{12,4},{16,8},{20,12},{24,16},{28,20},{1,25},{... | collective-permute-start | bytes 1572872 | tf_op jit(solution)/shard_map/ppermute | solution.py:262
  73.8 12.0 %attend1.1 = (bf16[128,2048]{1,0:T(8,128)(2,1)}, f32[2,128,512]{2,1,0:T(8,128)S(1)}, bf16[2,128,512]{2,1,0:T(8,128)(2,1)S(1)}, bf16[2,128,512]{2,1,0:T(8,128)(2,...) custom-call(s32[4]{0:T(128)S(1)} %copy-done.7, s32[1]{0:T(128)} %bitcast.block_ref, ...), custom_call_target="tpu_custom_call" | custom-call | flops 1677721600 | bytes 8388608 | tf_op jit(solution)/shard_map/attend1/pallas_call | solution.py:135
  89.4 1.7 collective-permute-start.17
  91.0 1.5 collective-permute-start.13
  95.4 1.7 slice.43
  97.1 1.9 collective-permute-start.12
  99.0 1.9 constant_dynamic-update-slice_fusion.10
  101.0 2.9 %collective-permute-done.13 = bf16[128,2048]{1,0:T(8,128)(2,1)} collective-permute-done((bf16[128,2048]{1,0:T(8,128)(2,1)}, bf16[128,2048]{1,0:T(8,128)(2,1)}, u32[]{:S(2)}, u32[]{:S(2)}) %collective-permute-start.13) | collective-permute-done | bytes 524320 | tf_op jit(solution)/shard_map/ppermute | solution.py:266
  103.8 2.8 collective-permute-start.14
  106.6 1.9 constant_dynamic-update-slice_fusion.9
  111.0 1.9 constant_dynamic-update-slice_fusion.6
  112.9 1.9 constant_dynamic-update-slice_fusion.5
  115.6 2.6 collective-permute-done.15
  119.9 4.3 %fusion.8 = bf16[1024,1024]{1,0:T(8,128)(2,1)S(1)} fusion(bf16[1024,1024]{1,0:T(8,128)(2,1)S(1)} %copy-done.19, bf16[1024,2048]{1,0:T(8,128)(2,1)} %constant_dynamic-update-slice_fusion.2.ua_ref), kind=kOutput, calls=%fused_computation.12 | convolution fusion | flops 2148532224 | bytes 6291456 | tf_op jit(solution)/shard_map/dot_general | solution.py:28
  124.3 8.5 %collective-permute-start.24 = (bf16[1024,1024]{1,0:T(8,128)(2,1)S(1)}, bf16[1024,1024]{1,0:T(8,128)(2,1)S(1)}, u32[]{:S(2)}, u32[]{:S(2)}) collective-permute-start(bf16[1024,1024]{1,0:T(8,128)(2,1)S(1)} %fusion.8), channel_id=1, source_target_pairs={{0,32},{32,0},{64,96},{96,64},{1,33},{33,1},{65,97},{97,65},{2,34}... | collective-permute-start | bytes 6291464 | tf_op jit(solution)/shard_map/ppermute | solution.py:318
  134.1 1.3 collective-permute-start.6
  138.0 5.8 %collective-permute-done.5 = bf16[2,128,512]{2,1,0:T(8,128)(2,1)S(1)} collective-permute-done((bf16[2,128,512]{2,1,0:T(8,128)(2,1)S(1)}, bf16[2,128,512]{2,1,0:T(8,128)(2,1)S(1)}, u32[]{:S(2)}, u32[]{:S(2)}) %collective-permute-start.5) | collective-permute-done | bytes 262176 | tf_op jit(solution)/shard_map/ppermute | solution.py:344
  143.7 4.2 %collective-permute-start.19 = (bf16[128,2048]{1,0:T(8,128)(2,1)S(1)}, bf16[128,2048]{1,0:T(8,128)(2,1)S(1)}, u32[]{:S(2)}, u32[]{:S(2)}) collective-permute-start(bf16[128,2048]{1,0:T(8,128)(2,1)S(1)} %collective-permute-done.17), channel_id=1, source_target_pairs={{0,8},{4,12},{8,16},{12,20},{16,24},{20,28},{24,0},{28,4},{1,9},{5... | collective-permute-start | bytes 1572872 | tf_op jit(solution)/shard_map/ppermute | solution.py:258
  147.9 6.5 %collective-permute-done.6 = bf16[2,128,512]{2,1,0:T(8,128)(2,1)S(1)} collective-permute-done((bf16[2,128,512]{2,1,0:T(8,128)(2,1)S(1)}, bf16[2,128,512]{2,1,0:T(8,128)(2,1)S(1)}, u32[]{:S(2)}, u32[]{:S(2)}) %collective-permute-start.6) | collective-permute-done | bytes 262176 | tf_op jit(solution)/shard_map/ppermute | solution.py:344
  154.4 6.9 %collective-permute-start.18 = (bf16[128,2048]{1,0:T(8,128)(2,1)S(1)}, bf16[128,2048]{1,0:T(8,128)(2,1)S(1)}, u32[]{:S(2)}, u32[]{:S(2)}) collective-permute-start(bf16[128,2048]{1,0:T(8,128)(2,1)S(1)} %collective-permute-done.17), channel_id=1, source_target_pairs={{0,24},{4,28},{8,0},{12,4},{16,8},{20,12},{24,16},{28,20},{1,25},{... | collective-permute-start | bytes 1572872 | tf_op jit(solution)/shard_map/ppermute | solution.py:262
  161.3 1.7 collective-permute-start.22
  164.0 2.2 collective-permute-start.20
  167.1 4.4 %collective-permute-done.18 = bf16[128,2048]{1,0:T(8,128)(2,1)S(1)} collective-permute-done((bf16[128,2048]{1,0:T(8,128)(2,1)S(1)}, bf16[128,2048]{1,0:T(8,128)(2,1)S(1)}, u32[]{:S(2)}, u32[]{:S(2)}) %collective-permute-start.18) | collective-permute-done | bytes 524320 | tf_op jit(solution)/shard_map/ppermute | solution.py:262
  171.5 2.9 %collective-permute-start.21 = (bf16[64,2048]{1,0:T(8,128)(2,1)S(1)}, bf16[64,2048]{1,0:T(8,128)(2,1)S(1)}, u32[]{:S(2)}, u32[]{:S(2)}) collective-permute-start(bf16[64,2048]{1,0:T(8,128)(2,1)S(1)} %slice.45), channel_id=1, source_target_pairs={{0,24},{4,28},{8,0},{12,4},{16,8},{20,12},{24,16},{28,20},{1,25},{... | collective-permute-start | bytes 786440 | tf_op jit(solution)/shard_map/ppermute | solution.py:262
  174.5 5.0 %collective-permute-start.23 = (bf16[128,2048]{1,0:T(8,128)(2,1)S(1)}, bf16[128,2048]{1,0:T(8,128)(2,1)S(1)}, u32[]{:S(2)}, u32[]{:S(2)}) collective-permute-start(bf16[128,2048]{1,0:T(8,128)(2,1)S(1)} %collective-permute-done.22), channel_id=1, source_target_pairs={{0,24},{4,28},{8,0},{12,4},{16,8},{20,12},{24,16},{28,20},{1,25},{... | collective-permute-start | bytes 1572872 | tf_op jit(solution)/shard_map/ppermute | solution.py:262
  181.9 3.8 %add_convert_fusion.1 = bf16[1024,1024]{1,0:T(8,128)(2,1)} fusion(bf16[1024,1024]{1,0:T(8,128)(2,1)S(1)} %collective-permute-done.24, bf16[1024,1024]{1,0:T(8,128)(2,1)S(1)} %copy-done.19, bf16[1024,2048]{1,0:T(8,128)(2,1)S(1)} %copy-done.5), kind=kOutput, calls=%fused_computation.3 | convolution fusion | flops 2150629376 | bytes 8388608 | tf_op jit(solution)/shard_map/dot_general | solution.py:28
  187.7 3.4 %collective-permute-done.23 = bf16[128,2048]{1,0:T(8,128)(2,1)S(1)} collective-permute-done((bf16[128,2048]{1,0:T(8,128)(2,1)S(1)}, bf16[128,2048]{1,0:T(8,128)(2,1)S(1)}, u32[]{:S(2)}, u32[]{:S(2)}) %collective-permute-start.23) | collective-permute-done | bytes 524320 | tf_op jit(solution)/shard_map/ppermute | solution.py:262
  192.0 6.7 %collective-permute-done.25 = bf16[128,2048]{1,0:T(8,128)(2,1)S(1)} collective-permute-done((bf16[128,2048]{1,0:T(8,128)(2,1)S(1)}, bf16[128,2048]{1,0:T(8,128)(2,1)S(1)}, u32[]{:S(2)}, u32[]{:S(2)}) %collective-permute-start.25) | collective-permute-done | bytes 524320 | tf_op jit(solution)/shard_map/ppermute | solution.py:266
  200.4 2.8 %collective-permute-start.27 = (bf16[2048,1024]{1,0:T(8,128)(2,1)}, bf16[2048,1024]{1,0:T(8,128)(2,1)}, u32[]{:S(2)}, u32[]{:S(2)}) collective-permute-start(bf16[2048,1024]{1,0:T(8,128)(2,1)} %all-gather.2.cloned.1.call-done.own_ref), channel_id=1, source_target_pairs={{0,32},{32,0},{64,96},{96,64},{1,33},{33,1},{65,97},{97,65},{2,34}... | collective-permute-start | bytes 12582920 | tf_op jit(solution)/shard_map/ppermute | solution.py:348
  203.2 6.0 %fusion.11 = bf16[1024,1024]{1,0:T(8,128)(2,1)} fusion(bf16[1024,1024]{1,0:T(8,128)(2,1)} %reorder.1, bf16[1024,2048]{1,0:T(8,128)(2,1)} %constant_dynamic-update-slice_fusion.11.ub_ref), kind=kOutput, calls=%fused_computation.13 | convolution fusion | flops 2148532224 | bytes 6291456 | tf_op jit(solution)/shard_map/dot_general | solution.py:28
  209.2 4.4 %all-to-all-start = ((bf16[8,128,1024]{2,1,0:T(8,128)(2,1)}), bf16[8,128,1024]{2,1,0:T(8,128)(2,1)}, u32[]{:S(2)}, u32[]{:S(2)}) async-start(bf16[8,128,1024]{2,1,0:T(8,128)(2,1)} %bitcast.32), calls=%async_computation | async-start | bytes 4194304 | tf_op jit(solution)/shard_map/all_to_all | solution.py:322
  213.7 6.6 %add_convert_fusion = bf16[1024,1024]{1,0:T(8,128)(2,1)} fusion(bf16[1024,1024]{1,0:T(8,128)(2,1)} %collective-permute-done.28, bf16[1024,1024]{1,0:T(8,128)(2,1)} %reorder.1, bf16[1024,2048]{1,0:T(8,128)(2,1)} %constant_dynamic-update-slice_fusion.11.ub_ref), kind=kOutput, calls=%fused_computation.1 | convolution fusion | flops 2150629376 | bytes 8388608 | tf_op jit(solution)/shard_map/dot_general | solution.py:28
  220.3 19.5 %all-to-all-done = bf16[8,128,1024]{2,1,0:T(8,128)(2,1)} async-done(((bf16[8,128,1024]{2,1,0:T(8,128)(2,1)}), bf16[8,128,1024]{2,1,0:T(8,128)(2,1)}, u32[]{:S(2)}, u32[]{:S(2)}) %all-to-all-start) | async-done | bytes 2097184 | tf_op jit(solution)/shard_map/all_to_all | solution.py:322
  239.8 4.6 %all-to-all-start.1 = ((bf16[8,128,1024]{2,1,0:T(8,128)(2,1)}), bf16[8,128,1024]{2,1,0:T(8,128)(2,1)}, u32[]{:S(2)}, u32[]{:S(2)}) async-start(bf16[8,128,1024]{2,1,0:T(8,128)(2,1)} %bitcast.33), calls=%async_computation.1 | async-start | bytes 4194304 | tf_op jit(solution)/shard_map/all_to_all | solution.py:322
  245.2 2.0 convert_reduce_fusion.1
  247.2 2.2 copy-done.6
  249.4 2.2 copy-done.10
  251.6 16.8 %project.1 = bf16[1024,1024]{1,0:T(8,128)(2,1)} custom-call(s32[1]{0:T(128)} %bitcast.9.core_ref, s32[8]{0:T(128)S(1)} %copy-done.9, bf16[1024,2048]{1,0:T(8,128)(2,1)S(1)} %copy-done.6, bf16[1024,2048]{1,0:T(8,128)(2,1)} %constant_dynamic-update-slice_fusion.11.ub_ref, bf16[2048,1024]{1,0:T(8,128)(2,1)S(1)} %copy-done.10, ...), custom_call_target="tpu_custom_call" | custom-call | flops 8589934592 | bytes 18874368 | tf_op jit(solution)/shard_map/project/pallas_call | solution.py:211
  268.3 1.9 all-to-all-done.1
  270.3 2.0 convert_reduce_fusion
  (98 shorter events, 30.1 us)
Async XLA Ops:
  7.2 85.4 %copy-start = (bf16[1024,1024]{1,0:T(8,128)(2,1)S(1)}, bf16[1024,1024]{1,0:T(8,128)(2,1)}, u32[]{:S(2)}) copy-start(bf16[1024,1024]{1,0:T(8,128)(2,1)} %param.13) | copy-start | bytes 6291460
  7.2 27.0 %copy-start.8 = (s32[1,32]{1,0:T(1,128)S(1)}, s32[1,32]{1,0:T(1,128)}, u32[]{:S(2)}) copy-start(s32[1,32]{1,0:T(1,128)} %param.14) | copy-start | bytes 388
  7.2 27.0 %copy-start.7 = (s32[4]{0:T(128)S(1)}, s32[4]{0:T(128)}, u32[]{:S(2)}) copy-start(s32[4]{0:T(128)} %order_ref.3) | copy-start | bytes 52
  7.2 27.0 %copy-start.1 = (bf16[128,4096]{1,0:T(8,128)(2,1)S(1)}, bf16[128,4096]{1,0:T(8,128)(2,1)}, u32[]{:S(2)}) copy-start(bf16[128,4096]{1,0:T(8,128)(2,1)} %refs_3_.3) | copy-start | bytes 3145732
  7.2 193.2 %all-gather.2.cloned.1.call-start = ((), (), s32[]{:S(2)}) async-start(), calls=%async_computation.2 | async-start | bytes 5242880 | tf_op jit(solution)/shard_map/all_gather | solution.py:334
  9.2 24.9 %collective-permute-start = (bf16[128,1024]{1,0:T(8,128)(2,1)S(1)}, bf16[128,1024]{1,0:T(8,128)(2,1)}, u32[]{:S(2)}, u32[]{:S(2)}) collective-permute-start(bf16[128,1024]{1,0:T(8,128)(2,1)S(1)} %constant_dynamic-update-slice_fusion.refs_12_.refs_17_), channel_id=1, source_target_pairs={{0,4},{1,5},{2,6},{3,7},{4,8},{5,9},{6,10},{7,11},{8,12},{9,13},{1... | collective-permute-start | bytes 786440 | tf_op jit(solution)/shard_map/ppermute | solution.py:296
  15.6 18.6 %collective-permute-start.1 = (bf16[128,1024]{1,0:T(8,128)(2,1)S(1)}, bf16[128,1024]{1,0:T(8,128)(2,1)}, u32[]{:S(2)}, u32[]{:S(2)}) collective-permute-start(bf16[128,1024]{1,0:T(8,128)(2,1)S(1)} %constant_dynamic-update-slice_fusion.refs_12_.refs_17_), channel_id=1, source_target_pairs={{0,3},{1,4},{2,5},{3,6},{4,7},{5,8},{6,9},{7,10},{8,11},{9,12},{10... | collective-permute-start | bytes 786440 | tf_op jit(solution)/shard_map/ppermute | solution.py:296
  21.9 12.2 %collective-permute-start.2 = (bf16[128,1024]{1,0:T(8,128)(2,1)S(1)}, bf16[128,1024]{1,0:T(8,128)(2,1)}, u32[]{:S(2)}, u32[]{:S(2)}) collective-permute-start(bf16[128,1024]{1,0:T(8,128)(2,1)S(1)} %constant_dynamic-update-slice_fusion.refs_12_.refs_17_), channel_id=1, source_target_pairs={{0,2},{1,3},{2,4},{3,5},{4,6},{5,7},{6,8},{7,9},{8,10},{9,11},{10,... | collective-permute-start | bytes 786440 | tf_op jit(solution)/shard_map/ppermute | solution.py:296
  24.2 9.9 %collective-permute-start.3 = (bf16[128,1024]{1,0:T(8,128)(2,1)S(1)}, bf16[128,1024]{1,0:T(8,128)(2,1)}, u32[]{:S(2)}, u32[]{:S(2)}) collective-permute-start(bf16[128,1024]{1,0:T(8,128)(2,1)S(1)} %constant_dynamic-update-slice_fusion.refs_12_.refs_17_), channel_id=1, source_target_pairs={{0,1},{1,2},{2,3},{3,4},{4,5},{5,6},{6,7},{7,8},{8,9},{9,10},{10,1... | collective-permute-start | bytes 786440 | tf_op jit(solution)/shard_map/ppermute | solution.py:296
  34.2 1.2 copy-start.2
  45.7 1.4 collective-permute-start.4
  47.2 46.4 %collective-permute-start.10 = (bf16[128,2048]{1,0:T(8,128)(2,1)}, bf16[128,2048]{1,0:T(8,128)(2,1)}, u32[]{:S(2)}, u32[]{:S(2)}) collective-permute-start(bf16[128,2048]{1,0:T(8,128)(2,1)} %collective-permute-done.4), channel_id=1, source_target_pairs={{0,8},{4,12},{8,16},{12,20},{16,24},{20,28},{24,0},{28,4},{1,9},{5... | collective-permute-start | bytes 1572872 | tf_op jit(solution)/shard_map/ppermute | solution.py:258
  70.0 25.4 %collective-permute-start.9 = (bf16[128,2048]{1,0:T(8,128)(2,1)}, bf16[128,2048]{1,0:T(8,128)(2,1)}, u32[]{:S(2)}, u32[]{:S(2)}) collective-permute-start(bf16[128,2048]{1,0:T(8,128)(2,1)} %collective-permute-done.4), channel_id=1, source_target_pairs={{0,24},{4,28},{8,0},{12,4},{16,8},{20,12},{24,16},{28,20},{1,25},{... | collective-permute-start | bytes 1572872 | tf_op jit(solution)/shard_map/ppermute | solution.py:262
  85.8 0.8 copy-start.3
  89.4 11.6 %collective-permute-start.17 = (bf16[128,2048]{1,0:T(8,128)(2,1)}, bf16[128,2048]{1,0:T(8,128)(2,1)S(1)}, u32[]{:S(2)}, u32[]{:S(2)}) collective-permute-start(bf16[128,2048]{1,0:T(8,128)(2,1)} %get-tuple-element.35), channel_id=1, source_target_pairs={{0,0},{1,8},{2,16},{3,24},{4,4},{5,12},{6,20},{7,28},{8,9},{9,17},... | collective-permute-start | bytes 1572872 | tf_op jit(solution)/shard_map/ppermute | solution.py:330
  91.0 12.8 %collective-permute-start.13 = (bf16[128,2048]{1,0:T(8,128)(2,1)}, bf16[128,2048]{1,0:T(8,128)(2,1)}, u32[]{:S(2)}, u32[]{:S(2)}) collective-permute-start(bf16[128,2048]{1,0:T(8,128)(2,1)} %collective-permute-done.4), channel_id=1, source_target_pairs={{0,4},{4,0},{8,12},{12,8},{16,20},{20,16},{24,28},{28,24},{1,5},{5... | collective-permute-start | bytes 1572872 | tf_op jit(solution)/shard_map/ppermute | solution.py:266
  94.5 14.0 %collective-permute-start.11 = (bf16[64,2048]{1,0:T(8,128)(2,1)S(1)}, bf16[64,2048]{1,0:T(8,128)(2,1)S(1)}, u32[]{:S(2)}, u32[]{:S(2)}) collective-permute-start(bf16[64,2048]{1,0:T(8,128)(2,1)S(1)} %slice.42), channel_id=1, source_target_pairs={{0,8},{4,12},{8,16},{12,20},{16,24},{20,28},{24,0},{28,4},{1,9},{5... | collective-permute-start | bytes 786440 | tf_op jit(solution)/shard_map/ppermute | solution.py:258
  97.1 11.4 %collective-permute-start.12 = (bf16[64,2048]{1,0:T(8,128)(2,1)}, bf16[64,2048]{1,0:T(8,128)(2,1)S(1)}, u32[]{:S(2)}, u32[]{:S(2)}) collective-permute-start(bf16[64,2048]{1,0:T(8,128)(2,1)} %slice.43), channel_id=1, source_target_pairs={{0,24},{4,28},{8,0},{12,4},{16,8},{20,12},{24,16},{28,20},{1,25},{... | collective-permute-start | bytes 786440 | tf_op jit(solution)/shard_map/ppermute | solution.py:262
  100.9 19.0 %copy-start.19 = (bf16[1024,1024]{1,0:T(8,128)(2,1)S(1)}, bf16[1024,1024]{1,0:T(8,128)(2,1)}, u32[]{:S(2)}) copy-start(bf16[1024,1024]{1,0:T(8,128)(2,1)} %reorder.1) | copy-start | bytes 6291460
  103.8 10.9 %collective-permute-start.14 = (bf16[128,2048]{1,0:T(8,128)(2,1)}, bf16[128,2048]{1,0:T(8,128)(2,1)S(1)}, u32[]{:S(2)}, u32[]{:S(2)}) collective-permute-start(bf16[128,2048]{1,0:T(8,128)(2,1)} %collective-permute-done.13), channel_id=1, source_target_pairs={{0,24},{4,28},{8,0},{12,4},{16,8},{20,12},{24,16},{28,20},{1,25},{... | collective-permute-start | bytes 1572872 | tf_op jit(solution)/shard_map/ppermute | solution.py:262
  106.6 12.4 %collective-permute-start.16 = (bf16[128,2048]{1,0:T(8,128)(2,1)}, bf16[128,2048]{1,0:T(8,128)(2,1)S(1)}, u32[]{:S(2)}, u32[]{:S(2)}) collective-permute-start(bf16[128,2048]{1,0:T(8,128)(2,1)} %collective-permute-done.13), channel_id=1, source_target_pairs={{0,8},{4,12},{8,16},{12,20},{16,24},{20,28},{24,0},{28,4},{1,9},{5... | collective-permute-start | bytes 1572872 | tf_op jit(solution)/shard_map/ppermute | solution.py:258
  108.5 9.6 %collective-permute-start.15 = (bf16[128,2048]{1,0:T(8,128)(2,1)S(1)}, bf16[128,2048]{1,0:T(8,128)(2,1)S(1)}, u32[]{:S(2)}, u32[]{:S(2)}) collective-permute-start(bf16[128,2048]{1,0:T(8,128)(2,1)S(1)} %pad_maximum_fusion.1), channel_id=1, source_target_pairs={{0,4},{4,0},{8,12},{12,8},{16,20},{20,16},{24,28},{28,24},{1,5},{5... | collective-permute-start | bytes 1572872 | tf_op jit(solution)/shard_map/ppermute | solution.py:266
  119.9 12.9 %copy-start.18 = (bf16[2,128,512]{2,1,0:T(8,128)(2,1)S(1)}, bf16[2,128,512]{2,1,0:T(8,128)(2,1)}, u32[]{:S(2)}) copy-start(bf16[2,128,512]{2,1,0:T(8,128)(2,1)} %copy-done.17) | copy-start | bytes 786436
  119.9 14.1 %copy-start.16 = (bf16[2,128,512]{2,1,0:T(8,128)(2,1)S(1)}, bf16[2,128,512]{2,1,0:T(8,128)(2,1)}, u32[]{:S(2)}) copy-start(bf16[2,128,512]{2,1,0:T(8,128)(2,1)} %copy-done.15) | copy-start | bytes 786436
  119.9 15.5 %copy-start.14 = (bf16[2,128,512]{2,1,0:T(8,128)(2,1)S(1)}, bf16[2,128,512]{2,1,0:T(8,128)(2,1)}, u32[]{:S(2)}) copy-start(bf16[2,128,512]{2,1,0:T(8,128)(2,1)} %copy-done.13) | copy-start | bytes 786436
  119.9 16.8 %copy-start.12 = (bf16[2,128,512]{2,1,0:T(8,128)(2,1)S(1)}, bf16[2,128,512]{2,1,0:T(8,128)(2,1)}, u32[]{:S(2)}) copy-start(bf16[2,128,512]{2,1,0:T(8,128)(2,1)} %copy-done.11) | copy-start | bytes 786436
  119.9 43.1 %copy-start.4 = (f32[2,128,512]{2,1,0:T(8,128)S(1)}, f32[2,128,512]{2,1,0:T(8,128)}, u32[]{:S(2)}) copy-start(f32[2,128,512]{2,1,0:T(8,128)} %copy-done.3) | copy-start | bytes 1572868
  124.3 57.6 %copy-start.5 = (bf16[1024,2048]{1,0:T(8,128)(2,1)S(1)}, bf16[1024,2048]{1,0:T(8,128)(2,1)}, u32[]{:S(2)}) copy-start(bf16[1024,2048]{1,0:T(8,128)(2,1)} %constant_dynamic-update-slice_fusion.2.ua_ref) | copy-start | bytes 12582916
  124.3 57.6 %collective-permute-start.24 = (bf16[1024,1024]{1,0:T(8,128)(2,1)S(1)}, bf16[1024,1024]{1,0:T(8,128)(2,1)S(1)}, u32[]{:S(2)}, u32[]{:S(2)}) collective-permute-start(bf16[1024,1024]{1,0:T(8,128)(2,1)S(1)} %fusion.8), channel_id=1, source_target_pairs={{0,32},{32,0},{64,96},{96,64},{1,33},{33,1},{65,97},{97,65},{2,34}... | collective-permute-start | bytes 6291464 | tf_op jit(solution)/shard_map/ppermute | solution.py:318
  132.8 11.0 %collective-permute-start.5 = (bf16[2,128,512]{2,1,0:T(8,128)(2,1)S(1)}, bf16[2,128,512]{2,1,0:T(8,128)(2,1)S(1)}, u32[]{:S(2)}, u32[]{:S(2)}) collective-permute-start(bf16[2,128,512]{2,1,0:T(8,128)(2,1)S(1)} %copy-done.18), channel_id=1, source_target_pairs={{4,0},{5,1},{6,2},{7,3},{8,4},{9,5},{10,6},{11,7},{12,8},{13,9},{1... | collective-permute-start | bytes 786440 | tf_op jit(solution)/shard_map/ppermute | solution.py:344
  134.1 20.4 %collective-permute-start.6 = (bf16[2,128,512]{2,1,0:T(8,128)(2,1)S(1)}, bf16[2,128,512]{2,1,0:T(8,128)(2,1)S(1)}, u32[]{:S(2)}, u32[]{:S(2)}) collective-permute-start(bf16[2,128,512]{2,1,0:T(8,128)(2,1)S(1)} %copy-done.16), channel_id=1, source_target_pairs={{3,0},{4,1},{5,2},{6,3},{7,4},{8,5},{9,6},{10,7},{11,8},{12,9},{13... | collective-permute-start | bytes 786440 | tf_op jit(solution)/shard_map/ppermute | solution.py:344
  135.4 26.0 %collective-permute-start.7 = (bf16[2,128,512]{2,1,0:T(8,128)(2,1)S(1)}, bf16[2,128,512]{2,1,0:T(8,128)(2,1)S(1)}, u32[]{:S(2)}, u32[]{:S(2)}) collective-permute-start(bf16[2,128,512]{2,1,0:T(8,128)(2,1)S(1)} %copy-done.14), channel_id=1, source_target_pairs={{2,0},{3,1},{4,2},{5,3},{6,4},{7,5},{8,6},{9,7},{10,8},{11,9},{12,... | collective-permute-start | bytes 786440 | tf_op jit(solution)/shard_map/ppermute | solution.py:344
  136.7 26.4 %collective-permute-start.8 = (bf16[2,128,512]{2,1,0:T(8,128)(2,1)S(1)}, bf16[2,128,512]{2,1,0:T(8,128)(2,1)S(1)}, u32[]{:S(2)}, u32[]{:S(2)}) collective-permute-start(bf16[2,128,512]{2,1,0:T(8,128)(2,1)S(1)} %copy-done.12), channel_id=1, source_target_pairs={{1,0},{2,1},{3,2},{4,3},{5,4},{6,5},{7,6},{8,7},{9,8},{10,9},{11,1... | collective-permute-start | bytes 786440 | tf_op jit(solution)/shard_map/ppermute | solution.py:344
  143.7 20.3 %collective-permute-start.19 = (bf16[128,2048]{1,0:T(8,128)(2,1)S(1)}, bf16[128,2048]{1,0:T(8,128)(2,1)S(1)}, u32[]{:S(2)}, u32[]{:S(2)}) collective-permute-start(bf16[128,2048]{1,0:T(8,128)(2,1)S(1)} %collective-permute-done.17), channel_id=1, source_target_pairs={{0,8},{4,12},{8,16},{12,20},{16,24},{20,28},{24,0},{28,4},{1,9},{5... | collective-permute-start | bytes 1572872 | tf_op jit(solution)/shard_map/ppermute | solution.py:258
  154.4 17.1 %collective-permute-start.18 = (bf16[128,2048]{1,0:T(8,128)(2,1)S(1)}, bf16[128,2048]{1,0:T(8,128)(2,1)S(1)}, u32[]{:S(2)}, u32[]{:S(2)}) collective-permute-start(bf16[128,2048]{1,0:T(8,128)(2,1)S(1)} %collective-permute-done.17), channel_id=1, source_target_pairs={{0,24},{4,28},{8,0},{12,4},{16,8},{20,12},{24,16},{28,20},{1,25},{... | collective-permute-start | bytes 1572872 | tf_op jit(solution)/shard_map/ppermute | solution.py:262
  161.3 13.1 %collective-permute-start.22 = (bf16[128,2048]{1,0:T(8,128)(2,1)S(1)}, bf16[128,2048]{1,0:T(8,128)(2,1)S(1)}, u32[]{:S(2)}, u32[]{:S(2)}) collective-permute-start(bf16[128,2048]{1,0:T(8,128)(2,1)S(1)} %collective-permute-done.17), channel_id=1, source_target_pairs={{0,4},{4,0},{8,12},{12,8},{16,20},{20,16},{24,28},{28,24},{1,5},{5... | collective-permute-start | bytes 1572872 | tf_op jit(solution)/shard_map/ppermute | solution.py:266
  164.0 16.3 %collective-permute-start.20 = (bf16[64,2048]{1,0:T(8,128)(2,1)S(1)}, bf16[64,2048]{1,0:T(8,128)(2,1)S(1)}, u32[]{:S(2)}, u32[]{:S(2)}) collective-permute-start(bf16[64,2048]{1,0:T(8,128)(2,1)S(1)} %slice.44), channel_id=1, source_target_pairs={{0,8},{4,12},{8,16},{12,20},{16,24},{20,28},{24,0},{28,4},{1,9},{5... | collective-permute-start | bytes 786440 | tf_op jit(solution)/shard_map/ppermute | solution.py:258
  171.5 9.5 %collective-permute-start.21 = (bf16[64,2048]{1,0:T(8,128)(2,1)S(1)}, bf16[64,2048]{1,0:T(8,128)(2,1)S(1)}, u32[]{:S(2)}, u32[]{:S(2)}) collective-permute-start(bf16[64,2048]{1,0:T(8,128)(2,1)S(1)} %slice.45), channel_id=1, source_target_pairs={{0,24},{4,28},{8,0},{12,4},{16,8},{20,12},{24,16},{28,20},{1,25},{... | collective-permute-start | bytes 786440 | tf_op jit(solution)/shard_map/ppermute | solution.py:262
  174.5 16.7 %collective-permute-start.23 = (bf16[128,2048]{1,0:T(8,128)(2,1)S(1)}, bf16[128,2048]{1,0:T(8,128)(2,1)S(1)}, u32[]{:S(2)}, u32[]{:S(2)}) collective-permute-start(bf16[128,2048]{1,0:T(8,128)(2,1)S(1)} %collective-permute-done.22), channel_id=1, source_target_pairs={{0,24},{4,28},{8,0},{12,4},{16,8},{20,12},{24,16},{28,20},{1,25},{... | collective-permute-start | bytes 1572872 | tf_op jit(solution)/shard_map/ppermute | solution.py:262
  179.5 20.0 %collective-permute-start.26 = (bf16[128,2048]{1,0:T(8,128)(2,1)S(1)}, bf16[128,2048]{1,0:T(8,128)(2,1)S(1)}, u32[]{:S(2)}, u32[]{:S(2)}) collective-permute-start(bf16[128,2048]{1,0:T(8,128)(2,1)S(1)} %collective-permute-done.22), channel_id=1, source_target_pairs={{0,8},{4,12},{8,16},{12,20},{16,24},{20,28},{24,0},{28,4},{1,9},{5... | collective-permute-start | bytes 1572872 | tf_op jit(solution)/shard_map/ppermute | solution.py:258
  185.7 13.0 %collective-permute-start.25 = (bf16[128,2048]{1,0:T(8,128)(2,1)S(1)}, bf16[128,2048]{1,0:T(8,128)(2,1)S(1)}, u32[]{:S(2)}, u32[]{:S(2)}) collective-permute-start(bf16[128,2048]{1,0:T(8,128)(2,1)S(1)} %pad_maximum_fusion.2), channel_id=1, source_target_pairs={{0,4},{4,0},{8,12},{12,8},{16,20},{20,16},{24,28},{28,24},{1,5},{5... | collective-permute-start | bytes 1572872 | tf_op jit(solution)/shard_map/ppermute | solution.py:266
  200.4 46.8 %collective-permute-start.27 = (bf16[2048,1024]{1,0:T(8,128)(2,1)}, bf16[2048,1024]{1,0:T(8,128)(2,1)}, u32[]{:S(2)}, u32[]{:S(2)}) collective-permute-start(bf16[2048,1024]{1,0:T(8,128)(2,1)} %all-gather.2.cloned.1.call-done.own_ref), channel_id=1, source_target_pairs={{0,32},{32,0},{64,96},{96,64},{1,33},{33,1},{65,97},{97,65},{2,34}... | collective-permute-start | bytes 12582920 | tf_op jit(solution)/shard_map/ppermute | solution.py:348
  209.2 4.5 %collective-permute-start.28 = (bf16[1024,1024]{1,0:T(8,128)(2,1)}, bf16[1024,1024]{1,0:T(8,128)(2,1)}, u32[]{:S(2)}, u32[]{:S(2)}) collective-permute-start(bf16[1024,1024]{1,0:T(8,128)(2,1)} %fusion.11), channel_id=1, source_target_pairs={{0,32},{32,0},{64,96},{96,64},{1,33},{33,1},{65,97},{97,65},{2,34}... | collective-permute-start | bytes 6291464 | tf_op jit(solution)/shard_map/ppermute | solution.py:318
  209.2 30.6 %all-to-all-start = ((bf16[8,128,1024]{2,1,0:T(8,128)(2,1)}), bf16[8,128,1024]{2,1,0:T(8,128)(2,1)}, u32[]{:S(2)}, u32[]{:S(2)}) async-start(bf16[8,128,1024]{2,1,0:T(8,128)(2,1)} %bitcast.32), calls=%async_computation | async-start | bytes 4194304 | tf_op jit(solution)/shard_map/all_to_all | solution.py:322
  220.3 26.9 %copy-start.9 = (s32[8]{0:T(128)S(1)}, s32[8]{0:T(128)}, u32[]{:S(2)}) copy-start(s32[8]{0:T(128)} %stack.35.idx_ref.arrival_ref) | copy-start | bytes 100
  239.8 30.5 %all-to-all-start.1 = ((bf16[8,128,1024]{2,1,0:T(8,128)(2,1)}), bf16[8,128,1024]{2,1,0:T(8,128)(2,1)}, u32[]{:S(2)}, u32[]{:S(2)}) async-start(bf16[8,128,1024]{2,1,0:T(8,128)(2,1)} %bitcast.33), calls=%async_computation.1 | async-start | bytes 4194304 | tf_op jit(solution)/shard_map/all_to_all | solution.py:322
  247.2 2.2 copy-start.6
  249.4 2.2 copy-start.10
  (4 other events, 2.8 us)
Sparse Core Ops, SparseCore 0:
  101.1 69.4 all-gather.1

commit v2 on v1

--- a/solution.py
+++ b/solution.py
@@ -173,29 +173,52 @@
     )(idx, x)
 
 
-def project_kernel(core_ref, arrival_ref, ua_ref, ub_ref, own_ref, other_ref, o_ref, acc_ref):
+def weight_kernel(*refs):
+    piece_refs, hidden_ref, o_ref = refs[:8], refs[8], refs[9]
+    used = jnp.concatenate([r[...] for r in piece_refs], axis=0)
+    o_ref[...] = dot(used, hidden_ref[...], (((0,), (0,)), ((), ()))).astype(BF)
+
+
+def weight_part(pieces, hidden, half):
+    features, (tokens, wide) = pieces[0].shape[1] // 2, hidden.shape
+    step = 4 * TB
+    steps = features // step
+    return pl.pallas_call(
+        weight_kernel,
+        grid=(steps,),
+        in_specs=[pl.BlockSpec((TB, step), lambda i: (0, i + half * steps))] * 8
+        + [pl.BlockSpec((tokens, wide), lambda i: (0, 0))],
+        out_specs=pl.BlockSpec((step, wide), lambda i: (i, 0)),
+        out_shape=jax.ShapeDtypeStruct((features, wide), BF),
+        compiler_params=pltpu.CompilerParams(vmem_limit_bytes=58 << 20),
+        cost_estimate=pl.CostEstimate(
+            flops=2 * features * tokens * wide, bytes_accessed=6 << 20, transcendentals=0
+        ),
+        name="weight_part",
+    )(*pieces, hidden)
+
+
+def project_kernel(core_ref, arrival_ref, *refs):
+    a_refs, b_refs = refs[:8], refs[8:16]
+    own_ref, other_ref, o_ref, acc_ref = refs[16:]
     step = pl.program_id(0)
 
-    def add(first, second):
-        for m in range(4):
-            rows = pl.ds(m * 2 * TB, 2 * TB)
-            term = dot(ua_ref[rows, :], first[...]) + dot(ub_ref[rows, :], second[...])
-
-            @pl.when(step == 0)
-            def _():
-                acc_ref[rows, :] = term
-
-            @pl.when(step > 0)
-            def _():
-                acc_ref[rows, :] += term
-
-    @pl.when(core_ref[0] == 0)
-    def _():
-        add(own_ref, other_ref)
-
-    @pl.when(core_ref[0] == 1)
-    def _():
-        add(other_ref, own_ref)
+    even = core_ref[0] == 0
+    first = jnp.where(even, own_ref[...], other_ref[...])
+    second = jnp.where(even, other_ref[...], own_ref[...])
+    for m in range(2):
+        rows = pl.ds(m * 4 * TB, 4 * TB)
+        left = jnp.concatenate([r[...] for r in a_refs[4 * m : 4 * m + 4]], axis=0)
+        right = jnp.concatenate([r[...] for r in b_refs[4 * m : 4 * m + 4]], axis=0)
+        term = dot(left, first) + dot(right, second)
+
+        @pl.when(step == 0)
+        def _():
+            acc_ref[rows, :] = term
+
+        @pl.when(step > 0)
+        def _():
+            acc_ref[rows, :] += term
 
     @pl.when(step == pl.num_programs(0) - 1)
     def _():
@@ -204,32 +227,38 @@
             o_ref[pl.ds(at, TB), :] = acc_ref[pl.ds(i * TB, TB), :].astype(BF)
 
 
-def project(used_a, used_b, w_own, w_other, core, arrival):
-    tokens, wide = used_a.shape[0], w_own.shape[1]
-    used_spec = pl.BlockSpec((tokens, 4 * TB), lambda i, *_: (0, i))
-    w_spec = pl.BlockSpec((4 * TB, wide), lambda i, core, _: (2 * (i % 2) + (core[0] + i // 2) % 2, 0))
+def project(pieces_a, pieces_b, w_own, w_other, core, arrival):
+    tokens, wide = 8 * TB, w_own.shape[1]
+    piece_spec = pl.BlockSpec((TB, 4 * TB), lambda i, *_: (0, i))
+    w_spec = pl.BlockSpec(
+        (4 * TB, wide), lambda i, core, _: (2 * (i % 2) + (core[0] + i // 2) % 2, 0)
+    )
     return pl.pallas_call(
         project_kernel,
         grid_spec=pltpu.PrefetchScalarGridSpec(
             num_scalar_prefetch=2,
             grid=(4,),
-            in_specs=[used_spec] * 2 + [w_spec] * 2,
+            in_specs=[piece_spec] * 16 + [w_spec] * 2,
             out_specs=pl.BlockSpec((tokens, wide), lambda i, *_: (0, 0)),
             scratch_shapes=[pltpu.VMEM((tokens, wide), F32)],
         ),
         out_shape=jax.ShapeDtypeStruct((tokens, wide), BF),
-        compiler_params=pltpu.CompilerParams(vmem_limit_bytes=40 << 20),
+        compiler_params=pltpu.CompilerParams(vmem_limit_bytes=58 << 20),
         cost_estimate=pl.CostEstimate(
             flops=2 * tokens * wide * 4096, bytes_accessed=18 << 20, transcendentals=0
         ),
         name="project",
-    )(core, arrival, used_a, used_b, w_own, w_other)
+    )(core, arrival, *pieces_a, *pieces_b, w_own, w_other)
 
 
 ROWCOL = ("row", "col")
 X_UP = [(r, (r + 2) % 8) for r in range(8)]
 X_DOWN = [(r, (r - 2) % 8) for r in range(8)]
 Y_SWAP = [(r, r ^ 1) for r in range(8)]
+NEAR_SWAP = [(r, r ^ 2) for r in range(4)]
+Z_UP = [(c, (c + 1) % 4) for c in range(4)]
+Z_DOWN = [(c, (c - 1) % 4) for c in range(4)]
+Z_FAR = [(c, (c + 2) % 4) for c in range(4)]
 CORE_SWAP = [(r, r ^ 1) for r in range(4)]
 ONE_CORE = [[4 * (2 * n + core) + c for n in range(2) for c in range(4)] for core in range(2)]
 
@@ -266,27 +295,24 @@
     return lax.ppermute(x, "row", Y_SWAP)
 
 
-def share(t0):
-    h = TB // 2
-    t1 = up(t0)
-    t3 = down(t0)
-    y0 = swap_y(t0)
-    t2 = jnp.concatenate([up(t1[:h]), down(t3[h:])], axis=0)
+def share_first(t0):
+    return t0, up(t0), down(t0), swap_y(t0)
+
+
+def share_rest(stage, far_up, *after):
+    t0, t1, t3, y0 = stage
+    t2 = up(t1) if far_up else down(t3)
     y1 = up(y0)
     y3 = down(y0)
-
-    def rest(*after):
-        y2 = swap_y(tie(t2, *after))
-        return jnp.concatenate([t0, t3, t2, t1, y0, y3, y2, y1], axis=0)
-
-    return rest
+    y2 = swap_y(tie(t2, *after))
+    return t0, t3, t2, t1, y0, y3, y2, y1
 
 
 def body(queries, keys, values, out_grad, hidden_in, q_weight, lengths, kv_order):
     row = lax.axis_index("row")
     col = lax.axis_index("col")
     rollout = lax.axis_index("rollout")
-    core = rollout % 2
+    core, near = rollout % 2, rollout // 2
     x, y = row // 2, row % 2
     block = (row * 4 + col).astype(jnp.int32).reshape(1)
     core1 = core.astype(jnp.int32).reshape(1)
@@ -308,15 +334,28 @@
     qb, own = outs[:2]
     back = outs[2:]
 
-    dims = (((0,), (0,)), ((), ()))
-
-    def send_part(used):
-        return dot(used[:, used.shape[1] // 2 :], hidden, dims).astype(BF)
-
-    def lower(used, send):
-        half = used.shape[1] // 2
+    def lower(used):
+        send = weight_part(used, hidden, 1)
         came = lax.ppermute(send, "rollout", CORE_SWAP)
-        return (dot(used[:, :half], hidden, dims) + came.astype(F32)).astype(BF)
+        keep = weight_part(used, tie(hidden, send), 0)
+        return (keep.astype(F32) + came.astype(F32)).astype(BF)
+
+    def collect_far(low):
+        low = low.reshape(2, 4, TB, wide)
+
+        def to_col(n):
+            return lax.dynamic_index_in_dim(low, (col + n) % 4, 1, keepdims=False)
+
+        rows = (
+            to_col(0).astype(F32)
+            + lax.ppermute(to_col(1), "col", Z_UP).astype(F32)
+            + lax.ppermute(to_col(3), "col", Z_DOWN).astype(F32)
+            + lax.ppermute(to_col(2), "col", Z_FAR).astype(F32)
+        )
+        other = lax.dynamic_index_in_dim(rows, 1 - near, 0, keepdims=False).astype(BF)
+        return lax.dynamic_index_in_dim(rows, near, 0, keepdims=False), lax.ppermute(
+            other, "rollout", NEAR_SWAP
+        )
 
     def collect(low):
         return lax.all_to_all(
@@ -333,25 +372,23 @@
     mine = tie(mine.reshape(4 * TB, wide), turn_b)
     w_own = lax.all_gather(mine, "col", axis=0, tiled=True)
 
-    rest_a = share(turn_a)
-    rest_b = share(turn_b)
-    used_a = rest_a()
-    send_a = send_part(used_a)
-    low_a = lower(used_a, send_a)
-    back = [tie(b, turn_a) for b in back]
+    first_a = share_first(turn_a)
+    first_b = share_first(turn_b)
+    used_a = share_rest(first_a, True, *first_b[1:3])
+    low_a = lower(used_a)
     total = own
     for b in range(BACK):
-        total = total + lax.ppermute(back[b], ROWCOL, shift(b - BACK)).astype(F32)
-    used_b = rest_b(low_a, total)
-    got_a = collect(low_a)
-    w_own = tie(w_own, used_b)
+        total = total + lax.ppermute(tie(back[b], turn_a), ROWCOL, shift(b - BACK)).astype(F32)
+    used_b = share_rest(first_b, False, low_a, total)
+    mine_a, came_a = collect_far(low_a)
+    *used_b, w_own, mine_a = lax.optimization_barrier((*used_b, w_own, mine_a))
     w_other = lax.ppermute(w_own, "rollout", CORE_SWAP)
-    send_b = send_part(used_b)
-    low_b = lower(used_b, send_b)
+    low_b = lower(used_b)
     got_b = collect(low_b)
     input_grad = project(used_a, used_b, w_own, w_other, core1, arrival)
     got_b = tie(got_b, input_grad)
-    weight_grad = jnp.concatenate([sum_rows(got_a), sum_rows(got_b)], axis=0)
+    came_a = tie(came_a, input_grad)
+    weight_grad = jnp.concatenate([mine_a + came_a.astype(F32), sum_rows(got_b)], axis=0)
     return (total[0], total[1], input_grad, weight_grad)
 
 

time: 281 us -> 275 us (0.979)
  Pallas kernels: 45.4 us -> 68.4 us
  matrix products: 20.7 us -> 0 us
  local copies, waits for them, and re-layouts: 35.3 us -> 17 us
  other arithmetic: 5.35 us -> 14.2 us
    ppermute x6 -> x5, waiting for transfers between devices: 0.79 us -> 34.4 us  [up(): return lax.ppermute(x, 'row', X_UP)]
    pallas_call x0 -> x4, Pallas kernels: none -> 23.4 us  [weight_part(): pl.pallas_call(weight_kernel, grid=(steps,), in_specs=[pl.BlockSpec((TB,...]
    dot_general x4 -> x0, matrix products: 20.7 us -> none  [dot(): return lax.dot_general(a, b, dims, preferred_element_type=F32)]
    unnamed x57 -> x63, local copies, waits for them, and re-layouts: 27.4 us -> 10.8 us
    all_to_all x2 -> x1, waiting for transfers between devices: 21.4 us -> 6.65 us  [collect(): lax.all_to_all(low, ('rollout', 'col'), 0, 0, axis_index_groups=ONE_CORE,...]
    ppermute x6 -> x5, starting transfers between devices: 30.2 us -> 19.6 us  [up(): return lax.ppermute(x, 'row', X_UP)]
    ppermute x4, starting transfers between devices: 4.52 us -> 13.5 us  [swap_y(): return lax.ppermute(x, 'row', Y_SWAP)]
    ppermute x6 -> x5, waiting for transfers between devices: 7.82 us -> 0.01 us  [down(): return lax.ppermute(x, 'row', X_DOWN)]
  transfers between devices with their start and end apart: 32 -> 33, of which waited for: 11 -> 9; matrix products, arithmetic and copies ran while one was open for 17% -> 7% of each run, Pallas kernels for 13% -> 21%
where the time goes in v2:
time: 275 us; the launch traced here: 272 us
  starting transfers between devices  103 us (37%)
  Pallas kernels  68.4 us (25%)
  waiting for transfers between devices  55.2 us (20%)
  local copies, waits for them, and re-layouts  17 us (6%)
  between operations  14.4 us (5%)
  other arithmetic  14.2 us (5%)
    ppermute x5, waiting for transfers between devices, up(): return lax.ppermute(x, 'row', X_UP)  34.4 us
    pallas_call x4, Pallas kernels, weight_part(): pl.pallas_call(weight_kernel, grid=(steps,), in_specs=[pl.BlockSpec((TB,...  23.4 us
    pallas_call x2, Pallas kernels, attend(): pl.pallas_call(functools.partial(attend_kernel, parity, first), grid_spec...  22.4 us
    ppermute x5, starting transfers between devices, down(): return lax.ppermute(x, 'row', X_DOWN)  19.9 us
    ppermute x5, starting transfers between devices, up(): return lax.ppermute(x, 'row', X_UP)  19.6 us
    ppermute x4, starting transfers between devices, body(): lax.ppermute(kv, ROWCOL, shift(n))  18.5 us
    pallas_call x1, Pallas kernels, project(): pl.pallas_call(project_kernel, grid_spec=pltpu.PrefetchScalarGridSpec(num...  16.2 us
    ppermute x4, starting transfers between devices, swap_y(): return lax.ppermute(x, 'row', Y_SWAP)  13.5 us
  transfers between devices with their start and end apart: 33, of which 9 were waited for; matrix products, arithmetic and copies ran while one was open for 7% of the time, Pallas kernels for 21%

profile of v2, /device:TPU:1, one launch (start us, length us, event | category | flops | bytes accessed | tf_op | source)
XLA Modules:
  0.0 272.2 jit_solution(5964581900189339108)
XLA Ops:
  9.2 5.1 %collective-permute-start.3 = (bf16[128,1024]{1,0:T(8,128)(2,1)S(1)}, bf16[128,1024]{1,0:T(8,128)(2,1)}, u32[]{:S(2)}, u32[]{:S(2)}) collective-permute-start(bf16[128,1024]{1,0:T(8,128)(2,1)S(1)} %constant_dynamic-update-slice_fusion.refs_12_.refs_17_), channel_id=1, source_target_pairs={{0,1},{1,2},{2,3},{3,4},{4,5},{5,6},{6,7},{7,8},{8,9},{9,10},{10,1... | collective-permute-start | bytes 786440 | tf_op jit(solution)/shard_map/ppermute | solution.py:322
  14.3 5.2 %collective-permute-start.2 = (bf16[128,1024]{1,0:T(8,128)(2,1)S(1)}, bf16[128,1024]{1,0:T(8,128)(2,1)}, u32[]{:S(2)}, u32[]{:S(2)}) collective-permute-start(bf16[128,1024]{1,0:T(8,128)(2,1)S(1)} %constant_dynamic-update-slice_fusion.refs_12_.refs_17_), channel_id=1, source_target_pairs={{0,2},{1,3},{2,4},{3,5},{4,6},{5,7},{6,8},{7,9},{8,10},{9,11},{10,... | collective-permute-start | bytes 786440 | tf_op jit(solution)/shard_map/ppermute | solution.py:322
  19.5 5.3 %collective-permute-start.1 = (bf16[128,1024]{1,0:T(8,128)(2,1)S(1)}, bf16[128,1024]{1,0:T(8,128)(2,1)}, u32[]{:S(2)}, u32[]{:S(2)}) collective-permute-start(bf16[128,1024]{1,0:T(8,128)(2,1)S(1)} %constant_dynamic-update-slice_fusion.refs_12_.refs_17_), channel_id=1, source_target_pairs={{0,3},{1,4},{2,5},{3,6},{4,7},{5,8},{6,9},{7,10},{8,11},{9,12},{10... | collective-permute-start | bytes 786440 | tf_op jit(solution)/shard_map/ppermute | solution.py:322
  24.8 2.9 %collective-permute-start = (bf16[128,1024]{1,0:T(8,128)(2,1)S(1)}, bf16[128,1024]{1,0:T(8,128)(2,1)}, u32[]{:S(2)}, u32[]{:S(2)}) collective-permute-start(bf16[128,1024]{1,0:T(8,128)(2,1)S(1)} %constant_dynamic-update-slice_fusion.refs_12_.refs_17_), channel_id=1, source_target_pairs={{0,4},{1,5},{2,6},{3,7},{4,8},{5,9},{6,10},{7,11},{8,12},{9,13},{1... | collective-permute-start | bytes 786440 | tf_op jit(solution)/shard_map/ppermute | solution.py:322
  28.3 6.4 %reorder.1.refs_8_ = bf16[1024,1024]{1,0:T(8,128)(2,1)} custom-call(s32[8]{0:T(128)} %stack.35.idx_ref.arrival_ref, bf16[1024,1024]{1,0:T(8,128)(2,1)} %x_ref.1), custom_call_target="tpu_custom_call" | custom-call | bytes 4194304 | tf_op jit(solution)/shard_map/reorder/pallas_call | solution.py:162
  34.8 1.2 copy-done.2
  36.0 10.3 %attend0.1 = (bf16[128,2048]{1,0:T(8,128)(2,1)S(1)}, f32[2,640,512]{2,1,0:T(8,128)}) custom-call(s32[4]{0:T(128)S(1)} %copy-done.5, s32[1]{0:T(128)} %bitcast.block_ref, s32[1]{0:T(128)} %bitcast.9.core_ref, s32[32]{0:T(128)S(1)} %bitcast.40, bf16[128,4096]{1,0:T(8,128)(2,1)S(1)} %copy-done.1, bf16[128,4096]{1,0:T(8,128)(2,1)S(1)} %copy-done.1, ...), custom_call_target="tpu_custom_call" | custom-call | flops 1677721600 | bytes 8388608 | tf_op jit(solution)/shard_map/attend0/pallas_call | solution.py:135
  47.0 12.1 %attend1.1 = (bf16[128,2048]{1,0:T(8,128)(2,1)}, f32[2,128,512]{2,1,0:T(8,128)S(1)}, bf16[2,128,512]{2,1,0:T(8,128)(2,1)S(1)}, bf16[2,128,512]{2,1,0:T(8,128)(2,...) custom-call(s32[4]{0:T(128)S(1)} %copy-done.5, s32[1]{0:T(128)} %bitcast.block_ref, ...), custom_call_target="tpu_custom_call" | custom-call | flops 1677721600 | bytes 8388608 | tf_op jit(solution)/shard_map/attend1/pallas_call | solution.py:135
  63.5 1.7 collective-permute-start.14
  67.1 16.6 %collective-permute-start.10 = (bf16[128,2048]{1,0:T(8,128)(2,1)}, bf16[128,2048]{1,0:T(8,128)(2,1)S(1)}, u32[]{:S(2)}, u32[]{:S(2)}) collective-permute-start(bf16[128,2048]{1,0:T(8,128)(2,1)} %copy-done.16), channel_id=1, source_target_pairs={{0,8},{4,12},{8,16},{12,20},{16,24},{20,28},{24,0},{28,4},{1,9},{5... | collective-permute-start | bytes 1572872 | tf_op jit(solution)/shard_map/ppermute | solution.py:287
  84.7 9.7 %collective-permute-start.16 = (bf16[128,2048]{1,0:T(8,128)(2,1)}, bf16[128,2048]{1,0:T(8,128)(2,1)S(1)}, u32[]{:S(2)}, u32[]{:S(2)}) collective-permute-start(bf16[128,2048]{1,0:T(8,128)(2,1)} %copy-done.17), channel_id=1, source_target_pairs={{0,24},{4,28},{8,0},{12,4},{16,8},{20,12},{24,16},{28,20},{1,25},{... | collective-permute-start | bytes 1572872 | tf_op jit(solution)/shard_map/ppermute | solution.py:291
  94.4 7.9 %collective-permute-done.10.refs_3_ = bf16[128,2048]{1,0:T(8,128)(2,1)S(1)} collective-permute-done((bf16[128,2048]{1,0:T(8,128)(2,1)}, bf16[128,2048]{1,0:T(8,128)(2,1)S(1)}, u32[]{:S(2)}, u32[]{:S(2)}) %collective-permute-start.10) | collective-permute-done | bytes 524320 | tf_op jit(solution)/shard_map/ppermute | solution.py:287
  103.1 1.9 collective-permute-start.9
  105.0 1.4 collective-permute-start.18
  106.5 1.2 collective-permute-start.13
  107.7 6.0 %collective-permute-done.15.refs_11_.refs_3_ = bf16[128,2048]{1,0:T(8,128)(2,1)S(1)} collective-permute-done((bf16[128,2048]{1,0:T(8,128)(2,1)}, bf16[128,2048]{1,0:T(8,128)(2,1)S(1)}, u32[]{:S(2)}, u32[]{:S(2)}) %collective-permute-start.15) | collective-permute-done | bytes 524320 | tf_op jit(solution)/shard_map/ppermute | solution.py:287
  113.7 11.2 %collective-permute-done.11.refs_2_ = bf16[128,2048]{1,0:T(8,128)(2,1)S(1)} collective-permute-done((bf16[128,2048]{1,0:T(8,128)(2,1)S(1)}, bf16[128,2048]{1,0:T(8,128)(2,1)S(1)}, u32[]{:S(2)}, u32[]{:S(2)}) %collective-permute-start.11) | collective-permute-done | bytes 524320 | tf_op jit(solution)/shard_map/ppermute | solution.py:287
  124.9 2.0 collective-permute-start.17
  126.9 9.2 %collective-permute-done.18.refs_7_ = bf16[128,2048]{1,0:T(8,128)(2,1)S(1)} collective-permute-done((bf16[128,2048]{1,0:T(8,128)(2,1)S(1)}, bf16[128,2048]{1,0:T(8,128)(2,1)S(1)}, u32[]{:S(2)}, u32[]{:S(2)}) %collective-permute-start.18) | collective-permute-done | bytes 524320 | tf_op jit(solution)/shard_map/ppermute | solution.py:287
  137.8 5.9 %weight_part.4 = bf16[1024,1024]{1,0:T(8,128)(2,1)} custom-call(bf16[128,2048]{1,0:T(8,128)(2,1)} %copy-done.16, bf16[128,2048]{1,0:T(8,128)(2,1)} %copy-done.25, bf16[128,2048]{1,0:T(8,128)(2,1)} %copy-done.24, bf16[128,2048]{1,0:T(8,128)(2,1)} %copy-done.19, bf16[128,2048]{1,0:T(8,128)(2,1)} %copy-done.20, bf16[128,2048]{1,0:T(8,128)(2,1)} %copy-done.27, ...), custom_call_target="tpu_custom_call" | custom-call | flops 2147483648 | bytes 6291456 | tf_op jit(solution)/shard_map/weight_part/pallas_call | solution.py:186
  143.7 3.9 %collective-permute-start.22 = (bf16[1024,1024]{1,0:T(8,128)(2,1)}, bf16[1024,1024]{1,0:T(8,128)(2,1)}, u32[]{:S(2)}, u32[]{:S(2)}) collective-permute-start(bf16[1024,1024]{1,0:T(8,128)(2,1)} %weight_part.4), channel_id=1, source_target_pairs={{0,32},{32,0},{64,96},{96,64},{1,33},{33,1},{65,97},{97,65},{2,34}... | collective-permute-start | bytes 6291464 | tf_op jit(solution)/shard_map/ppermute | solution.py:339
  147.6 1.4 collective-permute-start.5
  149.0 1.3 collective-permute-start.6
  150.3 1.3 collective-permute-start.7
  151.6 1.3 collective-permute-start.8
  152.9 5.8 %weight_part.5 = bf16[1024,1024]{1,0:T(8,128)(2,1)} custom-call(bf16[128,2048]{1,0:T(8,128)(2,1)} %copy-done.16, bf16[128,2048]{1,0:T(8,128)(2,1)} %copy-done.25, bf16[128,2048]{1,0:T(8,128)(2,1)} %copy-done.24, bf16[128,2048]{1,0:T(8,128)(2,1)} %copy-done.19, bf16[128,2048]{1,0:T(8,128)(2,1)} %copy-done.20, bf16[128,2048]{1,0:T(8,128)(2,1)} %copy-done.27, ...), custom_call_target="tpu_custom_call" | custom-call | flops 2147483648 | bytes 6291456 | tf_op jit(solution)/shard_map/weight_part/pallas_call | solution.py:186
  158.7 7.5 %collective-permute-start.20 = (bf16[128,2048]{1,0:T(8,128)(2,1)S(1)}, bf16[128,2048]{1,0:T(8,128)(2,1)}, u32[]{:S(2)}, u32[]{:S(2)}) collective-permute-start(bf16[128,2048]{1,0:T(8,128)(2,1)S(1)} %copy-done.18), channel_id=1, source_target_pairs={{0,4},{4,0},{8,12},{12,8},{16,20},{20,16},{24,28},{28,24},{1,5},{5... | collective-permute-start | bytes 1572872 | tf_op jit(solution)/shard_map/ppermute | solution.py:295
  166.2 3.2 %add_convert_fusion.1 = bf16[1024,1024]{1,0:T(8,128)(2,1)S(1)} fusion(bf16[1024,1024]{1,0:T(8,128)(2,1)} %collective-permute-done.22, bf16[1024,1024]{1,0:T(8,128)(2,1)} %weight_part.5), kind=kLoop, calls=%fused_computation.2 | loop fusion | flops 4194304 | bytes 6291456 | tf_op jit(solution)/shard_map/convert_element_type | solution.py:341
  169.5 5.2 %collective-permute-start.19 = (bf16[128,2048]{1,0:T(8,128)(2,1)S(1)}, bf16[128,2048]{1,0:T(8,128)(2,1)}, u32[]{:S(2)}, u32[]{:S(2)}) collective-permute-start(bf16[128,2048]{1,0:T(8,128)(2,1)S(1)} %copy-done.22), channel_id=1, source_target_pairs={{0,24},{4,28},{8,0},{12,4},{16,8},{20,12},{24,16},{28,20},{1,25},{... | collective-permute-start | bytes 1572872 | tf_op jit(solution)/shard_map/ppermute | solution.py:291
  176.2 1.9 collective-permute-start.27
  178.1 2.0 collective-permute-start.26
  180.1 2.0 convert_add_fusion.2
  182.1 5.0 %collective-permute-done.20.refs_12_.refs_4_ = bf16[128,2048]{1,0:T(8,128)(2,1)} collective-permute-done((bf16[128,2048]{1,0:T(8,128)(2,1)S(1)}, bf16[128,2048]{1,0:T(8,128)(2,1)}, u32[]{:S(2)}, u32[]{:S(2)}) %collective-permute-start.20) | collective-permute-done | bytes 524320 | tf_op jit(solution)/shard_map/ppermute | solution.py:295
  188.0 1.9 collective-permute-start.21
  190.6 3.0 %collective-permute-start.23 = (bf16[128,2048]{1,0:T(8,128)(2,1)}, bf16[128,2048]{1,0:T(8,128)(2,1)}, u32[]{:S(2)}, u32[]{:S(2)}) collective-permute-start(bf16[128,2048]{1,0:T(8,128)(2,1)} %collective-permute-done.19.refs_10_.refs_2_), channel_id=1, source_target_pairs={{0,4},{4,0},{8,12},{12,8},{16,20},{20,16},{24,28},{28,24},{1,5},{5... | collective-permute-start | bytes 1572872 | tf_op jit(solution)/shard_map/ppermute | solution.py:295
  193.6 6.1 %collective-permute-done.27 = bf16[2,128,1024]{2,1,0:T(8,128)(2,1)S(1)} collective-permute-done((bf16[2,128,1024]{2,1,0:T(8,128)(2,1)}, bf16[2,128,1024]{2,1,0:T(8,128)(2,1)S(1)}, u32[]{:S(2)}, u32[]{:S(2)}) %collective-permute-start.27) | collective-permute-done | bytes 524320 | tf_op jit(solution)/shard_map/ppermute | solution.py:353
  201.7 1.8 fusion.1
  204.5 9.8 %collective-permute-start.28 = (bf16[2048,1024]{1,0:T(8,128)(2,1)}, bf16[2048,1024]{1,0:T(8,128)(2,1)}, u32[]{:S(2)}, u32[]{:S(2)}) collective-permute-start(bf16[2048,1024]{1,0:T(8,128)(2,1)} %all-gather.2.cloned.1.call-done.refs_16_), channel_id=1, source_target_pairs={{0,32},{32,0},{64,96},{96,64},{1,33},{33,1},{65,97},{97,65},{2,34}... | collective-permute-start | bytes 12582920 | tf_op jit(solution)/shard_map/ppermute | solution.py:385
  214.2 5.8 %weight_part.6 = bf16[1024,1024]{1,0:T(8,128)(2,1)} custom-call(bf16[128,2048]{1,0:T(8,128)(2,1)} %copy-done.17, bf16[128,2048]{1,0:T(8,128)(2,1)} %copy-done.21, bf16[128,2048]{1,0:T(8,128)(2,1)} %collective-permute-done.19.refs_10_.refs_2_, bf16[128,2048]{1,0:T(8,128)(2,1)} %copy-done.23, bf16[128,2048]{1,0:T(8,128)(2,1)} %collective-permute-done.20.refs_12_.refs_4_, ...), custom_call_target="tpu_custom_call" | custom-call | flops 2147483648 | bytes 6291456 | tf_op jit(solution)/shard_map/weight_part/pallas_call | solution.py:186
  220.0 5.9 %weight_part.7 = bf16[1024,1024]{1,0:T(8,128)(2,1)} custom-call(bf16[128,2048]{1,0:T(8,128)(2,1)} %copy-done.17, bf16[128,2048]{1,0:T(8,128)(2,1)} %copy-done.21, bf16[128,2048]{1,0:T(8,128)(2,1)} %collective-permute-done.19.refs_10_.refs_2_, bf16[128,2048]{1,0:T(8,128)(2,1)} %copy-done.23, bf16[128,2048]{1,0:T(8,128)(2,1)} %collective-permute-done.20.refs_12_.refs_4_, ...), custom_call_target="tpu_custom_call" | custom-call | flops 2147483648 | bytes 6291456 | tf_op jit(solution)/shard_map/weight_part/pallas_call | solution.py:186
  225.9 4.0 %add_convert_fusion = bf16[1024,1024]{1,0:T(8,128)(2,1)} fusion(bf16[1024,1024]{1,0:T(8,128)(2,1)S(1)} %collective-permute-done.30, bf16[1024,1024]{1,0:T(8,128)(2,1)} %weight_part.7), kind=kLoop, calls=%fused_computation.1 | loop fusion | flops 4194304 | bytes 6291456 | tf_op jit(solution)/shard_map/convert_element_type | solution.py:341
  229.9 4.3 %all-to-all-start = ((bf16[8,128,1024]{2,1,0:T(8,128)(2,1)}), bf16[8,128,1024]{2,1,0:T(8,128)(2,1)}, u32[]{:S(2)}, u32[]{:S(2)}) async-start(bf16[8,128,1024]{2,1,0:T(8,128)(2,1)} %bitcast.44), calls=%async_computation | async-start | bytes 4194304 | tf_op jit(solution)/shard_map/all_to_all | solution.py:361
  234.2 1.9 slice_bitcast_fusion
  236.1 1.4 collective-permute-start.29
  237.6 16.2 %project.1 = bf16[1024,1024]{1,0:T(8,128)(2,1)} custom-call(s32[1]{0:T(128)} %bitcast.9.core_ref, s32[8]{0:T(128)} %stack.35.idx_ref.arrival_ref, bf16[128,2048]{1,0:T(8,128)(2,1)} %copy-done.16, bf16[128,2048]{1,0:T(8,128)(2,1)} %copy-done.25, bf16[128,2048]{1,0:T(8,128)(2,1)} %copy-done.24, bf16[128,2048]{1,0:T(8,128)(2,1)} %copy-done.19, ...), custom_call_target="tpu_custom_call" | custom-call | flops 8589934592 | bytes 18874368 | tf_op jit(solution)/shard_map/project/pallas_call | solution.py:236
  253.8 6.7 %all-to-all-done = bf16[8,128,1024]{2,1,0:T(8,128)(2,1)} async-done(((bf16[8,128,1024]{2,1,0:T(8,128)(2,1)}), bf16[8,128,1024]{2,1,0:T(8,128)(2,1)}, u32[]{:S(2)}, u32[]{:S(2)}) %all-to-all-start) | async-done | bytes 2097184 | tf_op jit(solution)/shard_map/all_to_all | solution.py:361
  260.4 2.0 convert_reduce_fusion
  262.5 1.8 collective-permute-done.29
  (104 shorter events, 20.2 us)
Async XLA Ops:
  7.2 58.0 %copy-start = (bf16[1024,1024]{1,0:T(8,128)(2,1)S(1)}, bf16[1024,1024]{1,0:T(8,128)(2,1)}, u32[]{:S(2)}) copy-start(bf16[1024,1024]{1,0:T(8,128)(2,1)} %param.13) | copy-start | bytes 6291460
  7.2 197.3 %all-gather.2.cloned.1.call-start = ((), (), s32[]{:S(2)}) async-start(), calls=%async_computation.1 | async-start | bytes 5242880 | tf_op jit(solution)/shard_map/all_gather | solution.py:373
  9.2 25.5 %collective-permute-start.3 = (bf16[128,1024]{1,0:T(8,128)(2,1)S(1)}, bf16[128,1024]{1,0:T(8,128)(2,1)}, u32[]{:S(2)}, u32[]{:S(2)}) collective-permute-start(bf16[128,1024]{1,0:T(8,128)(2,1)S(1)} %constant_dynamic-update-slice_fusion.refs_12_.refs_17_), channel_id=1, source_target_pairs={{0,1},{1,2},{2,3},{3,4},{4,5},{5,6},{6,7},{7,8},{8,9},{9,10},{10,1... | collective-permute-start | bytes 786440 | tf_op jit(solution)/shard_map/ppermute | solution.py:322
  14.3 20.4 %collective-permute-start.2 = (bf16[128,1024]{1,0:T(8,128)(2,1)S(1)}, bf16[128,1024]{1,0:T(8,128)(2,1)}, u32[]{:S(2)}, u32[]{:S(2)}) collective-permute-start(bf16[128,1024]{1,0:T(8,128)(2,1)S(1)} %constant_dynamic-update-slice_fusion.refs_12_.refs_17_), channel_id=1, source_target_pairs={{0,2},{1,3},{2,4},{3,5},{4,6},{5,7},{6,8},{7,9},{8,10},{9,11},{10,... | collective-permute-start | bytes 786440 | tf_op jit(solution)/shard_map/ppermute | solution.py:322
  19.5 15.2 %collective-permute-start.1 = (bf16[128,1024]{1,0:T(8,128)(2,1)S(1)}, bf16[128,1024]{1,0:T(8,128)(2,1)}, u32[]{:S(2)}, u32[]{:S(2)}) collective-permute-start(bf16[128,1024]{1,0:T(8,128)(2,1)S(1)} %constant_dynamic-update-slice_fusion.refs_12_.refs_17_), channel_id=1, source_target_pairs={{0,3},{1,4},{2,5},{3,6},{4,7},{5,8},{6,9},{7,10},{8,11},{9,12},{10... | collective-permute-start | bytes 786440 | tf_op jit(solution)/shard_map/ppermute | solution.py:322
  24.8 10.0 %collective-permute-start = (bf16[128,1024]{1,0:T(8,128)(2,1)S(1)}, bf16[128,1024]{1,0:T(8,128)(2,1)}, u32[]{:S(2)}, u32[]{:S(2)}) collective-permute-start(bf16[128,1024]{1,0:T(8,128)(2,1)S(1)} %constant_dynamic-update-slice_fusion.refs_12_.refs_17_), channel_id=1, source_target_pairs={{0,4},{1,5},{2,6},{3,7},{4,8},{5,9},{6,10},{7,11},{8,12},{9,13},{1... | collective-permute-start | bytes 786440 | tf_op jit(solution)/shard_map/ppermute | solution.py:322
  46.3 16.4 %collective-permute-start.4 = (bf16[128,2048]{1,0:T(8,128)(2,1)S(1)}, bf16[128,2048]{1,0:T(8,128)(2,1)S(1)}, u32[]{:S(2)}, u32[]{:S(2)}) collective-permute-start(bf16[128,2048]{1,0:T(8,128)(2,1)S(1)} %get-tuple-element.39), channel_id=1, source_target_pairs={{0,0},{1,8},{2,16},{3,24},{4,4},{5,12},{6,20},{7,28},{8,9},{9,17},... | collective-permute-start | bytes 1572872 | tf_op jit(solution)/shard_map/ppermute | solution.py:368
  63.5 2.7 %collective-permute-start.14 = (bf16[128,2048]{1,0:T(8,128)(2,1)}, bf16[128,2048]{1,0:T(8,128)(2,1)S(1)}, u32[]{:S(2)}, u32[]{:S(2)}) collective-permute-start(bf16[128,2048]{1,0:T(8,128)(2,1)} %get-tuple-element.48), channel_id=1, source_target_pairs={{0,0},{1,8},{2,16},{3,24},{4,4},{5,12},{6,20},{7,28},{8,9},{9,17},... | collective-permute-start | bytes 1572872 | tf_op jit(solution)/shard_map/ppermute | solution.py:369
  67.0 80.5 %copy-start.14 = (bf16[2,128,512]{2,1,0:T(8,128)(2,1)S(1)}, bf16[2,128,512]{2,1,0:T(8,128)(2,1)}, u32[]{:S(2)}) copy-start(bf16[2,128,512]{2,1,0:T(8,128)(2,1)} %copy-done.13) | copy-start | bytes 786436
  67.0 81.9 %copy-start.12 = (bf16[2,128,512]{2,1,0:T(8,128)(2,1)S(1)}, bf16[2,128,512]{2,1,0:T(8,128)(2,1)}, u32[]{:S(2)}) copy-start(bf16[2,128,512]{2,1,0:T(8,128)(2,1)} %copy-done.11) | copy-start | bytes 786436
  67.1 83.2 %copy-start.10 = (bf16[2,128,512]{2,1,0:T(8,128)(2,1)S(1)}, bf16[2,128,512]{2,1,0:T(8,128)(2,1)}, u32[]{:S(2)}) copy-start(bf16[2,128,512]{2,1,0:T(8,128)(2,1)} %copy-done.9) | copy-start | bytes 786436
  67.1 84.5 %copy-start.8 = (bf16[2,128,512]{2,1,0:T(8,128)(2,1)S(1)}, bf16[2,128,512]{2,1,0:T(8,128)(2,1)}, u32[]{:S(2)}) copy-start(bf16[2,128,512]{2,1,0:T(8,128)(2,1)} %copy-done.7) | copy-start | bytes 786436
  67.1 35.3 %collective-permute-start.10 = (bf16[128,2048]{1,0:T(8,128)(2,1)}, bf16[128,2048]{1,0:T(8,128)(2,1)S(1)}, u32[]{:S(2)}, u32[]{:S(2)}) collective-permute-start(bf16[128,2048]{1,0:T(8,128)(2,1)} %copy-done.16), channel_id=1, source_target_pairs={{0,8},{4,12},{8,16},{12,20},{16,24},{20,28},{24,0},{28,4},{1,9},{5... | collective-permute-start | bytes 1572872 | tf_op jit(solution)/shard_map/ppermute | solution.py:287
  83.6 21.4 %collective-permute-start.12 = (bf16[128,2048]{1,0:T(8,128)(2,1)}, bf16[128,2048]{1,0:T(8,128)(2,1)S(1)}, u32[]{:S(2)}, u32[]{:S(2)}) collective-permute-start(bf16[128,2048]{1,0:T(8,128)(2,1)} %copy-done.16), channel_id=1, source_target_pairs={{0,4},{4,0},{8,12},{12,8},{16,20},{20,16},{24,28},{28,24},{1,5},{5... | collective-permute-start | bytes 1572872 | tf_op jit(solution)/shard_map/ppermute | solution.py:295
  84.7 21.8 %collective-permute-start.16 = (bf16[128,2048]{1,0:T(8,128)(2,1)}, bf16[128,2048]{1,0:T(8,128)(2,1)S(1)}, u32[]{:S(2)}, u32[]{:S(2)}) collective-permute-start(bf16[128,2048]{1,0:T(8,128)(2,1)} %copy-done.17), channel_id=1, source_target_pairs={{0,24},{4,28},{8,0},{12,4},{16,8},{20,12},{24,16},{28,20},{1,25},{... | collective-permute-start | bytes 1572872 | tf_op jit(solution)/shard_map/ppermute | solution.py:291
  94.4 19.3 %collective-permute-start.15 = (bf16[128,2048]{1,0:T(8,128)(2,1)}, bf16[128,2048]{1,0:T(8,128)(2,1)S(1)}, u32[]{:S(2)}, u32[]{:S(2)}) collective-permute-start(bf16[128,2048]{1,0:T(8,128)(2,1)} %copy-done.17), channel_id=1, source_target_pairs={{0,8},{4,12},{8,16},{12,20},{16,24},{20,28},{24,0},{28,4},{1,9},{5... | collective-permute-start | bytes 1572872 | tf_op jit(solution)/shard_map/ppermute | solution.py:287
  102.3 35.4 %copy-start.19 = (bf16[128,2048]{1,0:T(8,128)(2,1)}, bf16[128,2048]{1,0:T(8,128)(2,1)S(1)}, u32[]{:S(2)}) copy-start(bf16[128,2048]{1,0:T(8,128)(2,1)S(1)} %collective-permute-done.10.refs_3_) | copy-start | bytes 1572868
  102.3 22.6 %collective-permute-start.11 = (bf16[128,2048]{1,0:T(8,128)(2,1)S(1)}, bf16[128,2048]{1,0:T(8,128)(2,1)S(1)}, u32[]{:S(2)}, u32[]{:S(2)}) collective-permute-start(bf16[128,2048]{1,0:T(8,128)(2,1)S(1)} %collective-permute-done.10.refs_3_), channel_id=1, source_target_pairs={{0,8},{4,12},{8,16},{12,20},{16,24},{20,28},{24,0},{28,4},{1,9},{5... | collective-permute-start | bytes 1572872 | tf_op jit(solution)/shard_map/ppermute | solution.py:287
  103.1 23.8 %collective-permute-start.9 = (bf16[128,2048]{1,0:T(8,128)(2,1)}, bf16[128,2048]{1,0:T(8,128)(2,1)S(1)}, u32[]{:S(2)}, u32[]{:S(2)}) collective-permute-start(bf16[128,2048]{1,0:T(8,128)(2,1)} %copy-done.16), channel_id=1, source_target_pairs={{0,24},{4,28},{8,0},{12,4},{16,8},{20,12},{24,16},{28,20},{1,25},{... | collective-permute-start | bytes 1572872 | tf_op jit(solution)/shard_map/ppermute | solution.py:291
  105.0 32.7 %copy-start.20 = (bf16[128,2048]{1,0:T(8,128)(2,1)}, bf16[128,2048]{1,0:T(8,128)(2,1)S(1)}, u32[]{:S(2)}) copy-start(bf16[128,2048]{1,0:T(8,128)(2,1)S(1)} %collective-permute-done.12.refs_4_) | copy-start | bytes 1572868
  105.0 31.1 %collective-permute-start.18 = (bf16[128,2048]{1,0:T(8,128)(2,1)S(1)}, bf16[128,2048]{1,0:T(8,128)(2,1)S(1)}, u32[]{:S(2)}, u32[]{:S(2)}) collective-permute-start(bf16[128,2048]{1,0:T(8,128)(2,1)S(1)} %collective-permute-done.12.refs_4_), channel_id=1, source_target_pairs={{0,8},{4,12},{8,16},{12,20},{16,24},{20,28},{24,0},{28,4},{1,9},{5... | collective-permute-start | bytes 1572872 | tf_op jit(solution)/shard_map/ppermute | solution.py:287
  106.5 37.2 %copy-start.21 = (bf16[128,2048]{1,0:T(8,128)(2,1)}, bf16[128,2048]{1,0:T(8,128)(2,1)S(1)}, u32[]{:S(2)}) copy-start(bf16[128,2048]{1,0:T(8,128)(2,1)S(1)} %collective-permute-done.16.refs_9_.refs_1_) | copy-start | bytes 1572868
  106.5 29.7 %collective-permute-start.13 = (bf16[128,2048]{1,0:T(8,128)(2,1)S(1)}, bf16[128,2048]{1,0:T(8,128)(2,1)S(1)}, u32[]{:S(2)}, u32[]{:S(2)}) collective-permute-start(bf16[128,2048]{1,0:T(8,128)(2,1)S(1)} %collective-permute-done.12.refs_4_), channel_id=1, source_target_pairs={{0,24},{4,28},{8,0},{12,4},{16,8},{20,12},{24,16},{28,20},{1,25},{... | collective-permute-start | bytes 1572872 | tf_op jit(solution)/shard_map/ppermute | solution.py:291
  113.7 30.0 %copy-start.23 = (bf16[128,2048]{1,0:T(8,128)(2,1)}, bf16[128,2048]{1,0:T(8,128)(2,1)S(1)}, u32[]{:S(2)}) copy-start(bf16[128,2048]{1,0:T(8,128)(2,1)S(1)} %collective-permute-done.15.refs_11_.refs_3_) | copy-start | bytes 1572868
  124.9 12.9 %copy-start.24 = (bf16[128,2048]{1,0:T(8,128)(2,1)}, bf16[128,2048]{1,0:T(8,128)(2,1)S(1)}, u32[]{:S(2)}) copy-start(bf16[128,2048]{1,0:T(8,128)(2,1)S(1)} %collective-permute-done.11.refs_2_) | copy-start | bytes 1572868
  124.9 12.8 %collective-permute-start.17 = (bf16[128,2048]{1,0:T(8,128)(2,1)S(1)}, bf16[128,2048]{1,0:T(8,128)(2,1)}, u32[]{:S(2)}, u32[]{:S(2)}) collective-permute-start(bf16[128,2048]{1,0:T(8,128)(2,1)S(1)} %collective-permute-done.11.refs_2_), channel_id=1, source_target_pairs={{0,4},{4,0},{8,12},{12,8},{16,20},{20,16},{24,28},{28,24},{1,5},{5... | collective-permute-start | bytes 1572872 | tf_op jit(solution)/shard_map/ppermute | solution.py:295
  143.7 15.1 %collective-permute-start.22 = (bf16[1024,1024]{1,0:T(8,128)(2,1)}, bf16[1024,1024]{1,0:T(8,128)(2,1)}, u32[]{:S(2)}, u32[]{:S(2)}) collective-permute-start(bf16[1024,1024]{1,0:T(8,128)(2,1)} %weight_part.4), channel_id=1, source_target_pairs={{0,32},{32,0},{64,96},{96,64},{1,33},{33,1},{65,97},{97,65},{2,34}... | collective-permute-start | bytes 6291464 | tf_op jit(solution)/shard_map/ppermute | solution.py:339
  147.6 11.2 %copy-start.18 = (bf16[128,2048]{1,0:T(8,128)(2,1)S(1)}, bf16[128,2048]{1,0:T(8,128)(2,1)}, u32[]{:S(2)}) copy-start(bf16[128,2048]{1,0:T(8,128)(2,1)} %copy-done.17) | copy-start | bytes 1572868
  147.6 21.9 %collective-permute-start.5 = (bf16[2,128,512]{2,1,0:T(8,128)(2,1)S(1)}, bf16[2,128,512]{2,1,0:T(8,128)(2,1)S(1)}, u32[]{:S(2)}, u32[]{:S(2)}) collective-permute-start(bf16[2,128,512]{2,1,0:T(8,128)(2,1)S(1)} %copy-done.14), channel_id=1, source_target_pairs={{4,0},{5,1},{6,2},{7,3},{8,4},{9,5},{10,6},{11,7},{12,8},{13,9},{1... | collective-permute-start | bytes 786440 | tf_op jit(solution)/shard_map/ppermute | solution.py:381
  149.0 26.6 %collective-permute-start.6 = (bf16[2,128,512]{2,1,0:T(8,128)(2,1)S(1)}, bf16[2,128,512]{2,1,0:T(8,128)(2,1)S(1)}, u32[]{:S(2)}, u32[]{:S(2)}) collective-permute-start(bf16[2,128,512]{2,1,0:T(8,128)(2,1)S(1)} %copy-done.12), channel_id=1, source_target_pairs={{3,0},{4,1},{5,2},{6,3},{7,4},{8,5},{9,6},{10,7},{11,8},{12,9},{13... | collective-permute-start | bytes 786440 | tf_op jit(solution)/shard_map/ppermute | solution.py:381
  150.3 25.9 %collective-permute-start.7 = (bf16[2,128,512]{2,1,0:T(8,128)(2,1)S(1)}, bf16[2,128,512]{2,1,0:T(8,128)(2,1)}, u32[]{:S(2)}, u32[]{:S(2)}) collective-permute-start(bf16[2,128,512]{2,1,0:T(8,128)(2,1)S(1)} %copy-done.10), channel_id=1, source_target_pairs={{2,0},{3,1},{4,2},{5,3},{6,4},{7,5},{8,6},{9,7},{10,8},{11,9},{12,... | collective-permute-start | bytes 786440 | tf_op jit(solution)/shard_map/ppermute | solution.py:381
  151.6 26.5 %collective-permute-start.8 = (bf16[2,128,512]{2,1,0:T(8,128)(2,1)S(1)}, bf16[2,128,512]{2,1,0:T(8,128)(2,1)}, u32[]{:S(2)}, u32[]{:S(2)}) collective-permute-start(bf16[2,128,512]{2,1,0:T(8,128)(2,1)S(1)} %copy-done.8), channel_id=1, source_target_pairs={{1,0},{2,1},{3,2},{4,3},{5,4},{6,5},{7,6},{8,7},{9,8},{10,9},{11,1... | collective-permute-start | bytes 786440 | tf_op jit(solution)/shard_map/ppermute | solution.py:381
  158.7 10.8 %copy-start.22 = (bf16[128,2048]{1,0:T(8,128)(2,1)S(1)}, bf16[128,2048]{1,0:T(8,128)(2,1)}, u32[]{:S(2)}) copy-start(bf16[128,2048]{1,0:T(8,128)(2,1)} %copy-done.21) | copy-start | bytes 1572868
  158.7 28.4 %collective-permute-start.20 = (bf16[128,2048]{1,0:T(8,128)(2,1)S(1)}, bf16[128,2048]{1,0:T(8,128)(2,1)}, u32[]{:S(2)}, u32[]{:S(2)}) collective-permute-start(bf16[128,2048]{1,0:T(8,128)(2,1)S(1)} %copy-done.18), channel_id=1, source_target_pairs={{0,4},{4,0},{8,12},{12,8},{16,20},{20,16},{24,28},{28,24},{1,5},{5... | collective-permute-start | bytes 1572872 | tf_op jit(solution)/shard_map/ppermute | solution.py:295
  169.4 12.6 %copy-start.15 = (bf16[1024,1024]{1,0:T(8,128)(2,1)}, bf16[1024,1024]{1,0:T(8,128)(2,1)S(1)}, u32[]{:S(2)}) copy-start(bf16[1024,1024]{1,0:T(8,128)(2,1)S(1)} %add_convert_fusion.1) | copy-start | bytes 6291460
  169.5 10.6 %copy-start.4 = (f32[2,128,512]{2,1,0:T(8,128)S(1)}, f32[2,128,512]{2,1,0:T(8,128)}, u32[]{:S(2)}) copy-start(f32[2,128,512]{2,1,0:T(8,128)} %copy-done.3) | copy-start | bytes 1572868
  169.5 18.5 %collective-permute-start.19 = (bf16[128,2048]{1,0:T(8,128)(2,1)S(1)}, bf16[128,2048]{1,0:T(8,128)(2,1)}, u32[]{:S(2)}, u32[]{:S(2)}) collective-permute-start(bf16[128,2048]{1,0:T(8,128)(2,1)S(1)} %copy-done.22), channel_id=1, source_target_pairs={{0,24},{4,28},{8,0},{12,4},{16,8},{20,12},{24,16},{28,20},{1,25},{... | collective-permute-start | bytes 1572872 | tf_op jit(solution)/shard_map/ppermute | solution.py:291
  175.6 14.2 %collective-permute-start.25 = (bf16[2,128,1024]{2,1,0:T(8,128)(2,1)S(1)}, bf16[2,128,1024]{2,1,0:T(8,128)(2,1)S(1)}, u32[]{:S(2)}, u32[]{:S(2)}) collective-permute-start(bf16[2,128,1024]{2,1,0:T(8,128)(2,1)S(1)} %get-tuple-element.66), channel_id=1, source_target_pairs={{0,1},{1,2},{2,3},{3,0},{4,5},{5,6},{6,7},{7,4},{8,9},{9,10},{10,1... | collective-permute-start | bytes 1572872 | tf_op jit(solution)/shard_map/ppermute | solution.py:351
  176.2 23.5 %collective-permute-start.27 = (bf16[2,128,1024]{2,1,0:T(8,128)(2,1)}, bf16[2,128,1024]{2,1,0:T(8,128)(2,1)S(1)}, u32[]{:S(2)}, u32[]{:S(2)}) collective-permute-start(bf16[2,128,1024]{2,1,0:T(8,128)(2,1)} %get-tuple-element.67), channel_id=1, source_target_pairs={{0,2},{1,3},{2,0},{3,1},{4,6},{5,7},{6,4},{7,5},{8,10},{9,11},{10,... | collective-permute-start | bytes 1572872 | tf_op jit(solution)/shard_map/ppermute | solution.py:353
  178.1 23.6 %collective-permute-start.26 = (bf16[2,128,1024]{2,1,0:T(8,128)(2,1)S(1)}, bf16[2,128,1024]{2,1,0:T(8,128)(2,1)}, u32[]{:S(2)}, u32[]{:S(2)}) collective-permute-start(bf16[2,128,1024]{2,1,0:T(8,128)(2,1)S(1)} %get-tuple-element.68), channel_id=1, source_target_pairs={{0,3},{1,0},{2,1},{3,2},{4,7},{5,4},{6,5},{7,6},{8,11},{9,8},{10,9... | collective-permute-start | bytes 1572872 | tf_op jit(solution)/shard_map/ppermute | solution.py:352
  187.1 17.3 %collective-permute-start.24 = (bf16[128,2048]{1,0:T(8,128)(2,1)}, bf16[128,2048]{1,0:T(8,128)(2,1)}, u32[]{:S(2)}, u32[]{:S(2)}) collective-permute-start(bf16[128,2048]{1,0:T(8,128)(2,1)} %collective-permute-done.20.refs_12_.refs_4_), channel_id=1, source_target_pairs={{0,8},{4,12},{8,16},{12,20},{16,24},{20,28},{24,0},{28,4},{1,9},{5... | collective-permute-start | bytes 1572872 | tf_op jit(solution)/shard_map/ppermute | solution.py:287
  188.0 16.5 %collective-permute-start.21 = (bf16[128,2048]{1,0:T(8,128)(2,1)}, bf16[128,2048]{1,0:T(8,128)(2,1)}, u32[]{:S(2)}, u32[]{:S(2)}) collective-permute-start(bf16[128,2048]{1,0:T(8,128)(2,1)} %collective-permute-done.20.refs_12_.refs_4_), channel_id=1, source_target_pairs={{0,24},{4,28},{8,0},{12,4},{16,8},{20,12},{24,16},{28,20},{1,25},{... | collective-permute-start | bytes 1572872 | tf_op jit(solution)/shard_map/ppermute | solution.py:291
  190.6 13.8 %collective-permute-start.23 = (bf16[128,2048]{1,0:T(8,128)(2,1)}, bf16[128,2048]{1,0:T(8,128)(2,1)}, u32[]{:S(2)}, u32[]{:S(2)}) collective-permute-start(bf16[128,2048]{1,0:T(8,128)(2,1)} %collective-permute-done.19.refs_10_.refs_2_), channel_id=1, source_target_pairs={{0,4},{4,0},{8,12},{12,8},{16,20},{20,16},{24,28},{28,24},{1,5},{5... | collective-permute-start | bytes 1572872 | tf_op jit(solution)/shard_map/ppermute | solution.py:295
  204.5 33.1 %collective-permute-start.28 = (bf16[2048,1024]{1,0:T(8,128)(2,1)}, bf16[2048,1024]{1,0:T(8,128)(2,1)}, u32[]{:S(2)}, u32[]{:S(2)}) collective-permute-start(bf16[2048,1024]{1,0:T(8,128)(2,1)} %all-gather.2.cloned.1.call-done.refs_16_), channel_id=1, source_target_pairs={{0,32},{32,0},{64,96},{96,64},{1,33},{33,1},{65,97},{97,65},{2,34}... | collective-permute-start | bytes 12582920 | tf_op jit(solution)/shard_map/ppermute | solution.py:385
  220.0 5.9 %collective-permute-start.30 = (bf16[1024,1024]{1,0:T(8,128)(2,1)}, bf16[1024,1024]{1,0:T(8,128)(2,1)S(1)}, u32[]{:S(2)}, u32[]{:S(2)}) collective-permute-start(bf16[1024,1024]{1,0:T(8,128)(2,1)} %weight_part.6), channel_id=1, source_target_pairs={{0,32},{32,0},{64,96},{96,64},{1,33},{33,1},{65,97},{97,65},{2,34}... | collective-permute-start | bytes 6291464 | tf_op jit(solution)/shard_map/ppermute | solution.py:339
  229.9 30.6 %all-to-all-start = ((bf16[8,128,1024]{2,1,0:T(8,128)(2,1)}), bf16[8,128,1024]{2,1,0:T(8,128)(2,1)}, u32[]{:S(2)}, u32[]{:S(2)}) async-start(bf16[8,128,1024]{2,1,0:T(8,128)(2,1)} %bitcast.44), calls=%async_computation | async-start | bytes 4194304 | tf_op jit(solution)/shard_map/all_to_all | solution.py:361
  236.1 28.1 %collective-permute-start.29 = (bf16[128,1024]{1,0:T(8,128)(2,1)S(1)}, bf16[128,1024]{1,0:T(8,128)(2,1)S(1)}, u32[]{:S(2)}, u32[]{:S(2)}) collective-permute-start(bf16[128,1024]{1,0:T(8,128)(2,1)S(1)} %fusion.2), channel_id=1, source_target_pairs={{0,64},{32,96},{64,0},{96,32},{1,65},{33,97},{65,1},{97,33},{2,66}... | collective-permute-start | bytes 786440 | tf_op jit(solution)/shard_map/ppermute | solution.py:356
  253.8 10.5 %copy-start.28 = (f32[128,1024]{1,0:T(8,128)S(1)}, f32[128,1024]{1,0:T(8,128)}, u32[]{:S(2)}) copy-start(f32[128,1024]{1,0:T(8,128)} %dynamic-slice_bitcast_fusion) | copy-start | bytes 1572868
  (16 other events, 38.4 us)
Sparse Core Ops, SparseCore 0:
  67.2 71.6 all-gather.1
